TPU v7x, 128 devices: a whole 4x4x4 slice. The times are simulated.
128 devices in a mesh: site: 8 (over x, core), sec: 16 (over z, y).
Axes of the slice: x: 4, y: 4, z: 4, core: 2. Of those that a mesh axis runs over, the one named last changes fastest.
Arguments:
- tensors: bfloat16 [8, 32, 4, 512, 512], P('site', 'sec'), as said below
- factors: float32 [8, 32, 512, 512], P('site', 'sec'), as said below
- sector_sizes: int32 [8, 32], replicated, may hold values from 384 to 512, as said below
- merging: int32 [8, 32, 4], replicated, may hold values from 0 to 31, as said below
Outputs:
- isometry: float32 [8, 32, 4, 512, 512], P('site', 'sec')
- factor_out: float32 [8, 32, 512, 512], P('site', 'sec')
Inputs may be any that keep to these rules, and one draw needn't show every extreme that they name: `sector_sizes`: every bond has one sector of exactly 512 states and one of exactly 384. For every site and physical state, merging maps the left sectors one to one onto the right sectors; the 8 blocks (left sector, physical state) of the left sectors that lie on one index of sec go to 8 different indices of sec, one block to each. `tensors`: zero outside the rows below the left sector's size and the columns below the right sector's size. `factors`: upper triangular with a positive diagonal inside the sector's size, the identity on its padding.
All inputs are finite; a program needn't handle non-finite values.
Results may differ from a plain program's by a relative error of at most 0.007.
Values may be sent and summed in bfloat16 or wider, within the bound.
No kernel may reach another device: no remote copies, remote signals or barrier semaphores. Data moves between devices by JAX's collectives and lax.ppermute only.
A program may use at most 192 MiB of HBM per device.

v0:
```python
import math

import jax
import jax.numpy as jnp
from jax import lax
from jax.sharding import PartitionSpec as P

ROUNDS = 3


def from_behind(shard, axis, by):
    size = lax.axis_size(axis)
    return lax.ppermute(shard, axis, [(i, (i + by) % size) for i in range(size)])


def routing_maps(merging_rows, sec_index, sec_groups, sec_local, phys_count):
    total_keys = sec_groups * sec_local * phys_count
    ordinal = jnp.arange(total_keys, dtype=jnp.int32)
    left_sector = ordinal // phys_count
    phys_index = ordinal % phys_count
    right_sector = merging_rows.reshape(total_keys)
    source = left_sector // sec_local
    target = right_sector // sec_local
    local_count = sec_local * phys_count
    peers = jnp.arange(sec_groups, dtype=jnp.int32)
    own_targets = lax.dynamic_slice_in_dim(target, sec_index * local_count, local_count)
    send_map = (peers[:, None] == own_targets[None, :]).astype(jnp.bfloat16)
    row_id = jnp.where(
        target == sec_index, (right_sector - sec_index * sec_local) * phys_count + phys_index, -1
    )
    wanted = (jnp.arange(local_count, dtype=jnp.int32)[:, None] == row_id[None, :]).astype(
        jnp.float32
    )
    placed = (source[:, None] == peers[None, :]).astype(jnp.float32)
    pick_map = jnp.dot(wanted, placed, preferred_element_type=jnp.float32).astype(jnp.bfloat16)
    return (send_map, pick_map)


def send_blocks(flattened, send_map):
    return jnp.dot(send_map, flattened, preferred_element_type=jnp.float32).astype(jnp.bfloat16)


def pick_blocks(received, pick_map):
    return jnp.dot(pick_map, received, preferred_element_type=jnp.float32).astype(jnp.bfloat16)


def route_products(products, send_map, pick_map):
    outgoing = send_blocks(products, send_map)
    received = lax.all_to_all(outgoing, "sec", split_axis=0, concat_axis=0, tiled=True)
    return pick_blocks(received, pick_map)


def body(tensors, factors, sector_sizes, merging):
    site_index = lax.axis_index("site")
    sec_index = lax.axis_index("sec")
    site_count = lax.axis_size("site")
    sec_groups = lax.axis_size("sec")
    blocks = tensors[0]
    sec_local, phys_count, block_size = (blocks.shape[0], blocks.shape[1], blocks.shape[3])
    local_count = sec_local * phys_count
    block_area = block_size * block_size
    merging_rows = lax.dynamic_index_in_dim(merging, site_index, 0, keepdims=False)
    next_widths = lax.dynamic_index_in_dim(
        sector_sizes, (site_index + 1) % site_count, 0, keepdims=False
    )
    widths = lax.dynamic_slice_in_dim(next_widths, sec_index * sec_local, sec_local)
    padding = (jnp.arange(block_size, dtype=jnp.int32)[None, :] >= widths[:, None]).astype(
        jnp.float32
    )
    identity = jnp.eye(block_size, dtype=jnp.float32)
    send_map, pick_map = routing_maps(merging_rows, sec_index, sec_groups, sec_local, phys_count)
    carried = factors[0]
    for step_index in range(ROUNDS):
        left_factor = carried.astype(jnp.bfloat16)
        products = jnp.einsum(
            "ajk,apkl->apjl", left_factor, blocks, preferred_element_type=jnp.float32
        ).astype(jnp.bfloat16)
        stacked = route_products(products.reshape(local_count, block_area), send_map, pick_map)
        stacked = stacked.reshape(sec_local, phys_count * block_size, block_size)
        gram_matrix = jnp.einsum(
            "brl,brm->blm", stacked, stacked, preferred_element_type=jnp.float32
        )
        gram_matrix = gram_matrix + identity[None] * padding[:, None, :]
        lower_factor = jnp.linalg.cholesky(gram_matrix)
        upper_factor = jnp.swapaxes(lower_factor, -1, -2)
        if step_index + 1 < ROUNDS:
            outgoing_factor = upper_factor.astype(jnp.bfloat16)
            carried = from_behind(outgoing_factor, "site", 1)
    solved = lax.linalg.triangular_solve(
        lower_factor, stacked.astype(jnp.float32), left_side=False, lower=True, transpose_a=True
    )
    isometry = (solved * math.sqrt(phys_count * block_size)).reshape(
        1, sec_local, phys_count, block_size, block_size
    )
    return (isometry, upper_factor[None])


def solution(mesh):
    in_specs = (P("site", "sec", None, None, None), P("site", "sec", None, None), P(), P())
    out_specs = (P("site", "sec", None, None, None), P("site", "sec", None, None))
    return jax.shard_map(body, mesh=mesh, in_specs=in_specs, out_specs=out_specs, check_vma=False)
```

profile of v0, /device:TPU:0, one launch (start us, length us, event | category | flops | bytes accessed | tf_op | source)
XLA Modules:
  0.0 1292.0 jit_solution(7343591570213793632)
XLA Ops:
  64.7 122.8 %all-to-all-done = bf16[16,2,131072]{2,1,0:T(2,128)(2,1)} async-done(((bf16[16,2,131072]{2,1,0:T(2,128)(2,1)}), bf16[16,2,131072]{2,1,0:T(2,128)(2,1)}, u32[]{:S(2)}, u32[]{:S(2)}) %all-to-all-start) | async-done | bytes 8388640 | tf_op jit(solution)/shard_map/all_to_all | solution.py:49
  238.2 23.5 %custom-call.42 = f32[2,128,128]{2,1,0:T(8,128)S(1)} custom-call(f32[2,128,128]{2,1,0:T(8,128)S(1)} %cholesky.586), custom_call_target="Cholesky" | custom-call | tf_op jit(solution)/shard_map/jit(cholesky)/cholesky | solution.py:84
  262.0 19.7 %custom-call.43 = f32[2,1,128,128]{2,3,1,0:T(8,128)S(1)} custom-call(f32[2,1,128,128]{3,2,1,0:T(8,128)S(1)} %select_bitcast_fusion.8), custom_call_target="InvertDiagBlocksLowerTriangular" | custom-call | tf_op jit(solution)/shard_map/jit(cholesky)/cholesky | solution.py:84
  284.7 23.9 %custom-call.44 = f32[2,128,128]{2,1,0:T(8,128)S(1)} custom-call(f32[2,128,128]{2,1,0:T(8,128)S(1)} %cholesky.590), custom_call_target="Cholesky" | custom-call | tf_op jit(solution)/shard_map/jit(cholesky)/cholesky | solution.py:84
  308.6 19.7 %custom-call.45 = f32[2,1,128,128]{2,3,1,0:T(8,128)S(1)} custom-call(f32[2,1,128,128]{3,2,1,0:T(8,128)S(1)} %get-tuple-element.60), custom_call_target="InvertDiagBlocksLowerTriangular" | custom-call | tf_op jit(solution)/shard_map/jit(cholesky)/cholesky | solution.py:84
  330.3 23.5 %custom-call.46 = f32[2,128,128]{2,1,0:T(8,128)S(1)} custom-call(f32[2,128,128]{2,1,0:T(8,128)S(1)} %cholesky.595), custom_call_target="Cholesky" | custom-call | tf_op jit(solution)/shard_map/jit(cholesky)/cholesky | solution.py:84
  353.7 19.8 %custom-call.47 = f32[2,1,128,128]{2,3,1,0:T(8,128)S(1)} custom-call(f32[2,1,128,128]{3,2,1,0:T(8,128)S(1)} %get-tuple-element.58), custom_call_target="InvertDiagBlocksLowerTriangular" | custom-call | tf_op jit(solution)/shard_map/jit(cholesky)/cholesky | solution.py:84
  375.4 23.7 %custom-call.48 = f32[2,128,128]{2,1,0:T(8,128)S(1)} custom-call(f32[2,128,128]{2,1,0:T(8,128)S(1)} %convolution_subtract_fusion.9), custom_call_target="Cholesky" | custom-call | tf_op jit(solution)/shard_map/jit(cholesky)/cholesky | solution.py:84
  450.7 100.3 %all_to_all.36 = bf16[16,2,131072]{2,1,0:T(2,128)(2,1)} all-to-all(bf16[16,2,131072]{2,1,0:T(2,128)(2,1)} %reshape.273), channel_id=1, replica_groups=mesh['site'=8,'sec'=16] {'sec'}, dimensions={0} | all-to-all | bytes 16777216 | tf_op jit(solution)/shard_map/all_to_all | solution.py:49
  602.1 23.5 %custom-call.49 = f32[2,128,128]{2,1,0:T(8,128)S(1)} custom-call(f32[2,128,128]{2,1,0:T(8,128)S(1)} %cholesky.599), custom_call_target="Cholesky" | custom-call | tf_op jit(solution)/shard_map/jit(cholesky)/cholesky | solution.py:84
  625.8 19.7 %custom-call.50 = f32[2,1,128,128]{2,3,1,0:T(8,128)S(1)} custom-call(f32[2,1,128,128]{3,2,1,0:T(8,128)S(1)} %select_bitcast_fusion.5), custom_call_target="InvertDiagBlocksLowerTriangular" | custom-call | tf_op jit(solution)/shard_map/jit(cholesky)/cholesky | solution.py:84
  648.6 23.7 %custom-call.51 = f32[2,128,128]{2,1,0:T(8,128)S(1)} custom-call(f32[2,128,128]{2,1,0:T(8,128)S(1)} %cholesky.603), custom_call_target="Cholesky" | custom-call | tf_op jit(solution)/shard_map/jit(cholesky)/cholesky | solution.py:84
  672.3 19.7 %custom-call.52 = f32[2,1,128,128]{2,3,1,0:T(8,128)S(1)} custom-call(f32[2,1,128,128]{3,2,1,0:T(8,128)S(1)} %get-tuple-element.55), custom_call_target="InvertDiagBlocksLowerTriangular" | custom-call | tf_op jit(solution)/shard_map/jit(cholesky)/cholesky | solution.py:84
  693.9 23.5 %custom-call.53 = f32[2,128,128]{2,1,0:T(8,128)S(1)} custom-call(f32[2,128,128]{2,1,0:T(8,128)S(1)} %cholesky.608), custom_call_target="Cholesky" | custom-call | tf_op jit(solution)/shard_map/jit(cholesky)/cholesky | solution.py:84
  717.4 20.1 %custom-call.54 = f32[2,1,128,128]{2,3,1,0:T(8,128)S(1)} custom-call(f32[2,1,128,128]{3,2,1,0:T(8,128)S(1)} %get-tuple-element.53), custom_call_target="InvertDiagBlocksLowerTriangular" | custom-call | tf_op jit(solution)/shard_map/jit(cholesky)/cholesky | solution.py:84
  739.3 23.6 %custom-call.55 = f32[2,128,128]{2,1,0:T(8,128)S(1)} custom-call(f32[2,128,128]{2,1,0:T(8,128)S(1)} %convolution_subtract_fusion.8), custom_call_target="Cholesky" | custom-call | tf_op jit(solution)/shard_map/jit(cholesky)/cholesky | solution.py:84
  819.5 120.9 %all-to-all-done.2 = bf16[16,2,131072]{2,1,0:T(2,128)(2,1)} async-done(((bf16[16,2,131072]{2,1,0:T(2,128)(2,1)}), bf16[16,2,131072]{2,1,0:T(2,128)(2,1)}, u32[]{:S(2)}, u32[]{:S(2)}) %all-to-all-start.2) | async-done | bytes 8388640 | tf_op jit(solution)/shard_map/all_to_all | solution.py:49
  991.5 23.5 %custom-call.56 = f32[2,128,128]{2,1,0:T(8,128)S(1)} custom-call(f32[2,128,128]{2,1,0:T(8,128)S(1)} %cholesky.612), custom_call_target="Cholesky" | custom-call | tf_op jit(solution)/shard_map/jit(cholesky)/cholesky | solution.py:84
  1044.7 23.7 %custom-call.58 = f32[2,128,128]{2,1,0:T(8,128)S(1)} custom-call(f32[2,128,128]{2,1,0:T(8,128)S(1)} %cholesky.616), custom_call_target="Cholesky" | custom-call | tf_op jit(solution)/shard_map/jit(cholesky)/cholesky | solution.py:84
  1068.4 19.7 %custom-call.59 = f32[2,1,128,128]{2,3,1,0:T(8,128)S(1)} custom-call(f32[2,1,128,128]{3,2,1,0:T(8,128)S(1)} %get-tuple-element.50), custom_call_target="InvertDiagBlocksLowerTriangular" | custom-call | tf_op jit(solution)/shard_map/jit(cholesky)/cholesky | solution.py:84
  1090.0 23.5 %custom-call.60 = f32[2,128,128]{2,1,0:T(8,128)S(1)} custom-call(f32[2,128,128]{2,1,0:T(8,128)S(1)} %cholesky.621), custom_call_target="Cholesky" | custom-call | tf_op jit(solution)/shard_map/jit(cholesky)/cholesky | solution.py:84
  1113.5 20.1 %custom-call.61 = f32[2,1,128,128]{2,3,1,0:T(8,128)S(1)} custom-call(f32[2,1,128,128]{3,2,1,0:T(8,128)S(1)} %get-tuple-element.48), custom_call_target="InvertDiagBlocksLowerTriangular" | custom-call | tf_op jit(solution)/shard_map/jit(cholesky)/cholesky | solution.py:84
  1135.4 23.5 %custom-call.62 = f32[2,128,128]{2,1,0:T(8,128)S(1)} custom-call(f32[2,128,128]{2,1,0:T(8,128)S(1)} %convolution_subtract_fusion.7), custom_call_target="Cholesky" | custom-call | tf_op jit(solution)/shard_map/jit(cholesky)/cholesky | solution.py:84
  1176.3 79.6 %custom-call.27 = f32[2,4,128,128]{2,3,1,0:T(8,128)S(1)} custom-call(f32[2,4,128,128]{3,2,1,0:T(8,128)} %bitcast.206), custom_call_target="InvertDiagBlocksLowerTriangular" | custom-call | tf_op jit(solution)/shard_map/triangular_solve | solution.py:89
  (159 shorter events, 439.8 us)
Async XLA Ops:
  0.6 0.7 copy-start
  55.1 132.4 %all-to-all-start = ((bf16[16,2,131072]{2,1,0:T(2,128)(2,1)}), bf16[16,2,131072]{2,1,0:T(2,128)(2,1)}, u32[]{:S(2)}, u32[]{:S(2)}) async-start(bf16[16,2,131072]{2,1,0:T(2,128)(2,1)} %reshape.271), calls=%async_computation | async-start | bytes 16777216 | tf_op jit(solution)/shard_map/all_to_all | solution.py:49
  64.4 162.5 %copy-start.7 = (f32[512,512]{0,1:T(8,128)}, f32[512,512]{0,1:T(8,128)S(1)}, u32[]{:S(2)}) copy-start(f32[512,512]{0,1:T(8,128)S(1)} %fusion.52) | copy-start | bytes 3145732
  236.9 1.3 copy-start.5
  399.9 15.4 %collective-permute-start = (bf16[2,512,512]{1,2,0:T(8,128)(2,1)S(1)}, bf16[2,512,512]{1,2,0:T(8,128)(2,1)S(1)}, u32[]{:S(2)}, u32[]{:S(2)}) collective-permute-start(bf16[2,512,512]{1,2,0:T(8,128)(2,1)S(1)} %fusion.44), channel_id=1, source_target_pairs={{0,16},{16,32},{32,48},{48,64},{64,80},{80,96},{96,112},{112,0},{1... | collective-permute-start | bytes 3145736 | tf_op jit(solution)/shard_map/ppermute | solution.py:13
  584.7 6.1 copy-start.8
  600.8 1.3 copy-start.6
  763.9 15.4 %collective-permute-start.1 = (bf16[2,512,512]{1,2,0:T(8,128)(2,1)S(1)}, bf16[2,512,512]{1,2,0:T(8,128)(2,1)S(1)}, u32[]{:S(2)}, u32[]{:S(2)}) collective-permute-start(bf16[2,512,512]{1,2,0:T(8,128)(2,1)S(1)} %fusion.45), channel_id=1, source_target_pairs={{0,16},{16,32},{32,48},{48,64},{64,80},{80,96},{96,112},{112,0},{1... | collective-permute-start | bytes 3145736 | tf_op jit(solution)/shard_map/ppermute | solution.py:13
  814.7 125.7 %all-to-all-start.2 = ((bf16[16,2,131072]{2,1,0:T(2,128)(2,1)}), bf16[16,2,131072]{2,1,0:T(2,128)(2,1)}, u32[]{:S(2)}, u32[]{:S(2)}) async-start(bf16[16,2,131072]{2,1,0:T(2,128)(2,1)} %reshape.275), calls=%async_computation.2 | async-start | bytes 16777216 | tf_op jit(solution)/shard_map/all_to_all | solution.py:49
  974.1 6.1 copy-start.9
  990.1 1.3 copy-start.4
  1263.7 7.9 copy-start.2
  1271.6 8.2 copy-start.3
  1285.9 5.9 copy-start.1
where the time goes:
time: 1300 us; the launch traced here: 1290 us
  other arithmetic  597 us (46%)
  waiting for transfers between devices  275 us (21%)
  local copies, waits for them, and re-layouts  153 us (12%)
  matrix products  153 us (12%)
  blocking collectives  100 us (8%)
  starting transfers between devices  13 us (1%)
    another operation x48, other arithmetic, body(): lower_factor = jnp.linalg.cholesky(gram_matrix)  462 us
    all_to_all x2, waiting for transfers between devices, route_products(): lax.all_to_all(outgoing, 'sec', split_axis=0, concat_axis=0, tiled=True)  244 us
    unnamed x30, local copies, waits for them, and re-layouts  105 us
    all_to_all x1, blocking collectives, route_products(): lax.all_to_all(outgoing, 'sec', split_axis=0, concat_axis=0, tiled=True)  100 us
    another operation x2, other arithmetic, body(): lax.linalg.triangular_solve(lower_factor, stacked.astype(jnp.float32), le...  79.6 us
    dot_general x3, matrix products, pick_blocks(): jnp.dot(pick_map, received, preferred_element_type=jnp.float32)  50.7 us
    all_to_all x3, other arithmetic, route_products(): lax.all_to_all(outgoing, 'sec', split_axis=0, concat_axis=0, tiled=True)  32.2 us
    ppermute x2, waiting for transfers between devices, from_behind(): lax.ppermute(shard, axis, [(i, (i + by) % size) for i in range(size)])  30.8 us
  transfers between devices with their start and end apart: 4, of which 4 were waited for; matrix products, arithmetic and copies ran while one was open for 0% of the time, Pallas kernels for 0%

commit v1 on v0

v1 whole, which is shorter than its diff:
```python
import functools
import math

import jax
import jax.numpy as jnp
from jax import lax
from jax.experimental import pallas as pl
from jax.experimental.pallas import tpu as pltpu
from jax.sharding import PartitionSpec as P

ROUNDS = 3
F32 = jnp.float32
BF16 = jnp.bfloat16
TILE = 128
HIGHEST = lax.Precision.HIGHEST


def contract(left, right, left_dim, right_dim, precision=None):
    dims = (((left_dim,), (right_dim,)), ((), ()))
    return lax.dot_general(left, right, dims, precision=precision, preferred_element_type=F32)


def from_behind(shard, axis, by):
    size = lax.axis_size(axis)
    return lax.ppermute(shard, axis, [(i, (i + by) % size) for i in range(size)])


def packed_starts(tiles):
    starts, total = [], 0
    for k in range(tiles):
        starts.append(total)
        total += tiles - k
    return starts, total


def pack_upper(square, tiles):
    pieces = []
    for k in range(tiles):
        for q in range(k, tiles):
            piece = square[k * TILE : (k + 1) * TILE, q * TILE : (q + 1) * TILE]
            pieces.append(piece.astype(BF16))
    return pieces


def place_tensor_kernel(slot_ref, block_ref, out_ref):
    out_ref[...] = block_ref[...]


def place_tensors(blocks, slots, groups):
    count, rows, columns = blocks.shape
    return pl.pallas_call(
        place_tensor_kernel,
        out_shape=jax.ShapeDtypeStruct((groups, rows, columns), blocks.dtype),
        grid_spec=pltpu.PrefetchScalarGridSpec(
            num_scalar_prefetch=1,
            grid=(count,),
            in_specs=[pl.BlockSpec((1, rows, columns), lambda g, slot: (g, 0, 0))],
            out_specs=pl.BlockSpec((1, rows, columns), lambda g, slot: (slot[g], 0, 0)),
        ),
        name="place_tensors",
    )(slots, blocks)


def place_packed(packed, slots, groups, phys_count):
    _, rows, columns = packed.shape
    count = slots.shape[0]
    return pl.pallas_call(
        place_tensor_kernel,
        out_shape=jax.ShapeDtypeStruct((groups, rows, columns), packed.dtype),
        grid_spec=pltpu.PrefetchScalarGridSpec(
            num_scalar_prefetch=1,
            grid=(count,),
            in_specs=[pl.BlockSpec((1, rows, columns), lambda g, slot: (g // phys_count, 0, 0))],
            out_specs=pl.BlockSpec((1, rows, columns), lambda g, slot: (slot[g], 0, 0)),
        ),
        name="place_packed",
    )(slots, packed)


def pack_kernel(tiles, factor_ref, out_ref):
    for index, piece in enumerate(pack_upper(factor_ref[0], tiles)):
        out_ref[0, index * TILE : (index + 1) * TILE, :] = piece


def pack_factors(factors):
    count, size, _ = factors.shape
    tiles = size // TILE
    _, total = packed_starts(tiles)
    return pl.pallas_call(
        functools.partial(pack_kernel, tiles),
        out_shape=jax.ShapeDtypeStruct((count, total * TILE, TILE), BF16),
        grid=(count,),
        in_specs=[pl.BlockSpec((1, size, size), lambda g: (g, 0, 0))],
        out_specs=pl.BlockSpec((1, total * TILE, TILE), lambda g: (g, 0, 0)),
        name="pack_factors",
    )(factors)


def product_kernel(tiles, phys_count, keep, source_ref, tensor_ref, factor_ref, gram_ref, *rest):
    starts, _ = packed_starts(tiles)
    step = pl.program_id(0)
    product_ref = rest[0]
    for k in range(tiles):
        row = jnp.concatenate(
            [
                factor_ref[0, (starts[k] + q - k) * TILE : (starts[k] + q - k + 1) * TILE, :]
                for q in range(k, tiles)
            ],
            axis=1,
        )
        part = contract(row, tensor_ref[0, k * TILE :, :], 1, 0)
        product_ref[0, k * TILE : (k + 1) * TILE, :] = part.astype(BF16)
    product = product_ref[0]
    gram = contract(product, product, 0, 0)

    @pl.when(step % phys_count == 0)
    def _():
        gram_ref[0] = gram

    @pl.when(step % phys_count != 0)
    def _():
        gram_ref[0] += gram


def products_and_gram(tensor_slots, factor_slots, sources, sec_local, phys_count, keep):
    _, size, _ = tensor_slots.shape
    _, packed_rows, _ = factor_slots.shape
    tiles = size // TILE
    count = sec_local * phys_count
    out_shape = [jax.ShapeDtypeStruct((sec_local, size, size), F32)]
    out_specs = [pl.BlockSpec((1, size, size), lambda g, source: (g // phys_count, 0, 0))]
    scratch = []
    if keep:
        out_shape.append(jax.ShapeDtypeStruct((count, size, size), BF16))
        out_specs.append(pl.BlockSpec((1, size, size), lambda g, source: (g, 0, 0)))
    else:
        scratch.append(pltpu.VMEM((1, size, size), BF16))
    return pl.pallas_call(
        functools.partial(product_kernel, tiles, phys_count, keep),
        out_shape=out_shape,
        grid_spec=pltpu.PrefetchScalarGridSpec(
            num_scalar_prefetch=1,
            grid=(count,),
            in_specs=[
                pl.BlockSpec((1, size, size), lambda g, source: (source[g], 0, 0)),
                pl.BlockSpec((1, packed_rows, TILE), lambda g, source: (source[g], 0, 0)),
            ],
            out_specs=out_specs,
            scratch_shapes=scratch,
        ),
        name="products_and_gram",
    )(sources, tensor_slots, factor_slots)


def factor_tile(stacks):
    done = [[] for _ in stacks]
    groups = TILE // 8
    for group in range(groups):
        rows = [[] for _ in stacks]
        for r in range(8):
            j = group * 8 + r
            for s, stack in enumerate(stacks):
                row = stack[group][r : r + 1, :]
                pivot = jnp.broadcast_to(row[:, j : j + 1], (1, TILE))
                rows[s].append(row * lax.rsqrt(pivot))
                if j < TILE - 1:
                    inverse = jnp.broadcast_to(1.0 / pivot, (8, TILE))
                    wide = jnp.broadcast_to(row, (8, TILE))
                    for i in range(group if r < 7 else group + 1, groups):
                        column = jnp.broadcast_to(stack[i][:, j : j + 1], (8, TILE))
                        stack[i] = stack[i] - column * wide * inverse
        for s in range(len(stacks)):
            done[s].append(jnp.concatenate(rows[s], axis=0))
    return done


def invert_tiles(uppers, row_id, column_id):
    inverses = []
    for upper in uppers:
        diagonal = jnp.sum(jnp.where(row_id == column_id, upper, 0.0), axis=0, keepdims=True)
        inverses.append(jnp.where(row_id == column_id, 1.0 / diagonal, 0.0))
    span = 1
    while span < TILE:
        pair = (row_id // (2 * span) == column_id // (2 * span)) & (
            row_id // span != column_id // span
        )
        inner = [
            contract(jnp.where(pair, upper, 0.0), inverse, 1, 0, HIGHEST)
            for upper, inverse in zip(uppers, inverses)
        ]
        inverses = [
            inverse - contract(inverse, part, 1, 0, HIGHEST)
            for inverse, part in zip(inverses, inner)
        ]
        span *= 2
    return inverses


def factor_kernel(count, tiles, final, scale, width_ref, gram_ref, *refs):
    if final:
        upper_ref, high_ref, low_ref, work, diag_inverse, full = refs
    else:
        packed_ref, work, diag_inverse = refs
        upper_ref = None
    size = tiles * TILE
    starts, _ = packed_starts(tiles)
    row_id = lax.broadcasted_iota(jnp.int32, (TILE, TILE), 0)
    column_id = lax.broadcasted_iota(jnp.int32, (TILE, TILE), 1)
    for s in range(count):
        work[s] = gram_ref[s]
        for k in range(tiles):
            lo, hi = k * TILE, (k + 1) * TILE
            on = (row_id == column_id) & (row_id + lo >= width_ref[s])
            work[s, lo:hi, lo:hi] = work[s, lo:hi, lo:hi] + jnp.where(on, 1.0, 0.0)
        if final:
            upper_ref[s] = jnp.zeros((size, size), F32)

    def step(p, carry):
        first = pl.multiple_of(p * TILE, TILE)
        stacks = []
        for s in range(count):
            stacks.append(
                [
                    work[s, pl.ds(pl.multiple_of(first + 8 * i, 8), 8), pl.ds(first, TILE)]
                    for i in range(TILE // 8)
                ]
            )
        uppers = [
            jnp.where(row_id <= column_id, jnp.concatenate(rows, axis=0), 0.0)
            for rows in factor_tile(stacks)
        ]
        inverses = invert_tiles(uppers, row_id, column_id)
        for s in range(count):
            diag_inverse[s, pl.ds(first, TILE), :] = inverses[s]
        for k in range(tiles):

            @pl.when(p == k)
            def _(k=k):
                lo, hi = k * TILE, (k + 1) * TILE
                for s in range(count):
                    if final:
                        upper_ref[s, lo:hi, lo:hi] = uppers[s]
                    else:
                        at = starts[k] * TILE
                        packed_ref[s, at : at + TILE, :] = uppers[s].astype(BF16)
                    if k + 1 == tiles:
                        continue
                    panel = contract(inverses[s], work[s, lo:hi, hi:], 0, 0, HIGHEST)
                    for q in range(k + 1, tiles):
                        left = (q - k - 1) * TILE
                        piece = panel[:, left : left + TILE]
                        if final:
                            upper_ref[s, lo:hi, q * TILE : (q + 1) * TILE] = piece
                        else:
                            at = (starts[k] + q - k) * TILE
                            packed_ref[s, at : at + TILE, :] = piece.astype(BF16)
                        here = slice(q * TILE, (q + 1) * TILE)
                        work[s, here, q * TILE :] = work[s, here, q * TILE :] - contract(
                            piece, panel[:, left:], 0, 0, HIGHEST
                        )

        return carry

    lax.fori_loop(0, tiles, step, 0)
    if final:
        for s in range(count):
            full[...] = jnp.zeros((size, size), F32)
            for k in range(tiles):
                lo, hi = k * TILE, (k + 1) * TILE
                full[lo:hi, lo:hi] = diag_inverse[s, lo:hi, :]
            span = TILE
            while span < size:
                for lo in range(0, size, 2 * span):
                    mid, hi = lo + span, lo + 2 * span
                    inner = contract(
                        upper_ref[s, lo:mid, mid:hi], full[mid:hi, mid:hi], 1, 0, HIGHEST
                    )
                    full[lo:mid, mid:hi] = -contract(full[lo:mid, lo:mid], inner, 1, 0, HIGHEST)
                span *= 2
            scaled = full[...] * scale
            high = scaled.astype(BF16)
            high_ref[s] = high
            low_ref[s] = (scaled - high.astype(F32)).astype(BF16)


def factorize(gram, widths, final, scale):
    count, size, _ = gram.shape
    tiles = size // TILE
    _, total = packed_starts(tiles)
    vmem = pl.BlockSpec(memory_space=pltpu.VMEM)
    scratch = [pltpu.VMEM((count, size, size), F32), pltpu.VMEM((count, size, TILE), F32)]
    if final:
        out_shape = [jax.ShapeDtypeStruct((count, size, size), t) for t in (F32, BF16, BF16)]
        scratch.append(pltpu.VMEM((size, size), F32))
    else:
        out_shape = [jax.ShapeDtypeStruct((count, total * TILE, TILE), BF16)]
    return pl.pallas_call(
        functools.partial(factor_kernel, count, tiles, final, scale),
        out_shape=out_shape,
        in_specs=[pl.BlockSpec(memory_space=pltpu.SMEM), vmem],
        out_specs=[vmem] * len(out_shape),
        scratch_shapes=scratch,
        name="factorize_last" if final else "factorize",
    )(widths, gram)


def isometry_kernel(product_ref, high_ref, low_ref, out_ref):
    product = product_ref[0]
    out_ref[0] = contract(product, high_ref[0], 1, 0) + contract(product, low_ref[0], 1, 0)


def isometries(products, high, low, phys_count):
    count, size, _ = products.shape
    square = (1, size, size)
    return pl.pallas_call(
        isometry_kernel,
        out_shape=jax.ShapeDtypeStruct((count, size, size), F32),
        grid=(count,),
        in_specs=[
            pl.BlockSpec(square, lambda g: (g, 0, 0)),
            pl.BlockSpec(square, lambda g: (g // phys_count, 0, 0)),
            pl.BlockSpec(square, lambda g: (g // phys_count, 0, 0)),
        ],
        out_specs=pl.BlockSpec(square, lambda g: (g, 0, 0)),
        name="isometries",
    )(products, high, low)


def body(tensors, factors, sector_sizes, merging):
    site_index = lax.axis_index("site")
    sec_index = lax.axis_index("sec")
    site_count = lax.axis_size("site")
    groups = lax.axis_size("sec")
    blocks = tensors[0]
    sec_local, phys_count, size = blocks.shape[0], blocks.shape[1], blocks.shape[3]
    count = sec_local * phys_count
    rows = lax.dynamic_index_in_dim(merging, site_index, 0, keepdims=False)
    next_widths = lax.dynamic_index_in_dim(
        sector_sizes, (site_index + 1) % site_count, 0, keepdims=False
    )
    first = sec_index * sec_local
    widths = lax.dynamic_slice_in_dim(next_widths, first, sec_local)
    slots = lax.dynamic_slice_in_dim(rows, first, sec_local).reshape(count) // sec_local
    wanted = rows[None] == (first + jnp.arange(sec_local, dtype=jnp.int32))[:, None, None]
    owner = jnp.arange(rows.shape[0], dtype=jnp.int32)[None, :, None] // sec_local
    sources = jnp.sum(jnp.where(wanted, owner, 0), axis=1).reshape(count)

    def exchange(slotted):
        return lax.all_to_all(slotted, "sec", split_axis=0, concat_axis=0, tiled=True)

    tensor_slots = exchange(place_tensors(blocks.reshape(count, size, size), slots, groups))
    packed = pack_factors(factors[0])
    scale = math.sqrt(phys_count * size)
    for round_index in range(ROUNDS):
        final = round_index + 1 == ROUNDS
        factor_slots = exchange(place_packed(packed, slots, groups, phys_count))
        gram, *products = products_and_gram(
            tensor_slots, factor_slots, sources, sec_local, phys_count, final
        )
        outs = factorize(gram, widths, final, scale)
        if not final:
            packed = from_behind(outs[0], "site", 1)
    upper, high, low = outs
    isometry = isometries(products[0], high, low, phys_count)
    return isometry.reshape(1, sec_local, phys_count, size, size), upper[None]


def solution(mesh):
    in_specs = (P("site", "sec", None, None, None), P("site", "sec", None, None), P(), P())
    out_specs = (P("site", "sec", None, None, None), P("site", "sec", None, None))
    return jax.shard_map(body, mesh=mesh, in_specs=in_specs, out_specs=out_specs, check_vma=False)
```

time: 1300 us -> 636 us (0.49)
  other arithmetic: 597 us -> 0.82 us
  Pallas kernels: 0 us -> 259 us
  matrix products: 153 us -> 0 us
  local copies, waits for them, and re-layouts: 153 us -> 4.58 us
  waiting for transfers between devices: 275 us -> 214 us
  blocking collectives: 100 us -> 132 us
    another operation x50 -> x0, other arithmetic: 542 us -> none  [the longest x48 462 us: body(): lower_factor = jnp.linalg.cholesky(gram_matrix)]
    pallas_call x0 -> x12, Pallas kernels: none -> 259 us  [the longest x3 189 us: factorize(): pl.pallas_call(functools.partial(factor_kernel, count, tiles, final, scal...]
    dot_general x13 -> x0, matrix products: 105 us -> none  [the longest x3 50.7 us: pick_blocks(): jnp.dot(pick_map, received, preferred_element_type=jnp.float32)]
    unnamed x30 -> x8, local copies, waits for them, and re-layouts: 105 us -> 2.38 us
    all_to_all x2, waiting for transfers between devices: 244 us -> 191 us  [exchange(): lax.all_to_all(slotted, 'sec', split_axis=0, concat_axis=0, tiled=True)]
    another operation x25 -> x0, matrix products: 47.2 us -> none  [the longest x7 27 us: body(): lax.linalg.triangular_solve(lower_factor, stacked.astype(jnp.float32), le...]
    all_to_all x3 -> x0, other arithmetic: 32.2 us -> none  [route_products(): lax.all_to_all(outgoing, 'sec', split_axis=0, concat_axis=0, tiled=True)]
    all_to_all x1 -> x2, blocking collectives: 100 us -> 132 us  [exchange(): lax.all_to_all(slotted, 'sec', split_axis=0, concat_axis=0, tiled=True)]
  transfers between devices with their start and end apart: 4 -> 4, of which waited for: 4 -> 4; matrix products, arithmetic and copies ran while one was open for 0% -> 0% of each run, Pallas kernels for 0% -> 1%
where the time goes in v1:
time: 636 us; the launch traced here: 626 us
  Pallas kernels  259 us (41%)
  waiting for transfers between devices  214 us (34%)
  blocking collectives  132 us (21%)
  starting transfers between devices  13.5 us (2%)
    all_to_all x2, waiting for transfers between devices, exchange(): lax.all_to_all(slotted, 'sec', split_axis=0, concat_axis=0, tiled=True)  191 us
    pallas_call x3, Pallas kernels, factorize(): pl.pallas_call(functools.partial(factor_kernel, count, tiles, final, scal...  189 us
    all_to_all x2, blocking collectives, exchange(): lax.all_to_all(slotted, 'sec', split_axis=0, concat_axis=0, tiled=True)  132 us
    pallas_call x3, Pallas kernels, products_and_gram(): pl.pallas_call(functools.partial(product_kernel, tiles, phys_count, keep)...  33.9 us
    ppermute x2, waiting for transfers between devices, from_behind(): lax.ppermute(shard, axis, [(i, (i + by) % size) for i in range(size)])  22.9 us
    pallas_call x3, Pallas kernels, place_packed(): pl.pallas_call(place_tensor_kernel, out_shape=jax.ShapeDtypeStruct((group...  15.8 us
    all_to_all x2, starting transfers between devices, exchange(): lax.all_to_all(slotted, 'sec', split_axis=0, concat_axis=0, tiled=True)  13.5 us
  transfers between devices with their start and end apart: 4, of which 4 were waited for; matrix products, arithmetic and copies ran while one was open for 0% of the time, Pallas kernels for 1%

profile of v1, /device:TPU:0, one launch (start us, length us, event | category | flops | bytes accessed | tf_op | source)
XLA Modules:
  0.0 625.5 jit_solution(1051888714910697338)
XLA Ops:
  0.7 0.7 copy-done
  2.2 2.3 pack_factors.1.block_ref
  4.5 5.3 place_packed.3
  9.8 8.2 %all-to-all-start.1 = ((bf16[16,1280,128]{2,1,0:T(8,128)(2,1)}), bf16[16,1280,128]{2,1,0:T(8,128)(2,1)}, u32[]{:S(2)}, u32[]{:S(2)}) async-start(bf16[16,1280,128]{2,1,0:T(8,128)(2,1)} %place_packed.3), calls=%async_computation.1 | async-start | bytes 10485760 | tf_op jit(solution)/shard_map/all_to_all | solution.py:349
  18.0 7.3 %place_tensors.1 = bf16[16,512,512]{2,1,0:T(8,128)(2,1)} custom-call(s32[8]{0:T(128)} %and_select_fusion.slot_ref, bf16[8,512,512]{2,1,0:T(8,128)(2,1)} %bitcast.9), custom_call_target="tpu_custom_call" | custom-call | tf_op jit(solution)/shard_map/place_tensors/pallas_call | solution.py:51
  25.3 71.0 %all-to-all-done.1.factor_ref = bf16[16,1280,128]{2,1,0:T(8,128)(2,1)} async-done(((bf16[16,1280,128]{2,1,0:T(8,128)(2,1)}), bf16[16,1280,128]{2,1,0:T(8,128)(2,1)}, u32[]{:S(2)}, u32[]{:S(2)}) %all-to-all-start.1) | async-done | bytes 5242912 | tf_op jit(solution)/shard_map/all_to_all | solution.py:349
  96.3 5.3 all-to-all-start
  102.5 1.3 dynamic-slice_bitcast_fusion.1.width_ref
  103.8 119.8 %all-to-all-done.tensor_ref = bf16[16,512,512]{2,1,0:T(8,128)(2,1)} async-done(((bf16[16,512,512]{2,1,0:T(8,128)(2,1)}), bf16[16,512,512]{2,1,0:T(8,128)(2,1)}, u32[]{:S(2)}, u32[]{:S(2)}) %all-to-all-start) | async-done | bytes 8388640 | tf_op jit(solution)/shard_map/all_to_all | solution.py:349
  223.6 11.0 %products_and_gram.3.gram_ref = f32[2,512,512]{2,1,0:T(8,128)} custom-call(s32[8]{0:T(128)} %reshape.57.source_ref, bf16[16,512,512]{2,1,0:T(8,128)(2,1)} %all-to-all-done.tensor_ref, bf16[16,1280,128]{2,1,0:T(8,128)(2,1)} %all-to-all-done.1.factor_ref), custom_call_target="tpu_custom_call" | custom-call | tf_op jit(solution)/shard_map/products_and_gram/pallas_call | solution.py:138
  234.7 61.8 %factorize.2 = bf16[2,1280,128]{2,1,0:T(8,128)(2,1)} custom-call(s32[2]{0:T(128)} %dynamic-slice_bitcast_fusion.1.width_ref, f32[2,512,512]{2,1,0:T(8,128)} %products_and_gram.3.gram_ref), custom_call_target="tpu_custom_call" | custom-call | tf_op jit(solution)/shard_map/factorize/pallas_call | solution.py:297
  296.5 11.4 %collective-permute-done.block_ref = bf16[2,1280,128]{2,1,0:T(8,128)(2,1)S(1)} collective-permute-done((bf16[2,1280,128]{2,1,0:T(8,128)(2,1)}, bf16[2,1280,128]{2,1,0:T(8,128)(2,1)S(1)}, u32[]{:S(2)}, u32[]{:S(2)}) %collective-permute-start) | collective-permute-done | bytes 655392 | tf_op jit(solution)/shard_map/ppermute | solution.py:25
  307.9 0.8 copy-done.3
  308.7 5.2 place_packed.4
  314.0 66.3 %all_to_all.20.factor_ref = bf16[16,1280,128]{2,1,0:T(8,128)(2,1)} all-to-all(bf16[16,1280,128]{2,1,0:T(8,128)(2,1)} %place_packed.4), channel_id=1, replica_groups=mesh['site'=8,'sec'=16] {'sec'}, dimensions={0} | all-to-all | bytes 10485760 | tf_op jit(solution)/shard_map/all_to_all | solution.py:349
  380.3 11.0 %products_and_gram.4.gram_ref = f32[2,512,512]{2,1,0:T(8,128)} custom-call(s32[8]{0:T(128)} %reshape.57.source_ref, bf16[16,512,512]{2,1,0:T(8,128)(2,1)} %all-to-all-done.tensor_ref, bf16[16,1280,128]{2,1,0:T(8,128)(2,1)} %all_to_all.20.factor_ref), custom_call_target="tpu_custom_call" | custom-call | tf_op jit(solution)/shard_map/products_and_gram/pallas_call | solution.py:138
  391.3 61.8 %factorize.3 = bf16[2,1280,128]{2,1,0:T(8,128)(2,1)} custom-call(s32[2]{0:T(128)} %dynamic-slice_bitcast_fusion.1.width_ref, f32[2,512,512]{2,1,0:T(8,128)} %products_and_gram.4.gram_ref), custom_call_target="tpu_custom_call" | custom-call | tf_op jit(solution)/shard_map/factorize/pallas_call | solution.py:297
  453.1 11.4 %collective-permute-done.1.block_ref = bf16[2,1280,128]{2,1,0:T(8,128)(2,1)S(1)} collective-permute-done((bf16[2,1280,128]{2,1,0:T(8,128)(2,1)}, bf16[2,1280,128]{2,1,0:T(8,128)(2,1)S(1)}, u32[]{:S(2)}, u32[]{:S(2)}) %collective-permute-start.1) | collective-permute-done | bytes 655392 | tf_op jit(solution)/shard_map/ppermute | solution.py:25
  464.5 0.8 copy-done.2
  465.4 5.2 place_packed.5
  470.6 66.2 %all_to_all.21.factor_ref = bf16[16,1280,128]{2,1,0:T(8,128)(2,1)} all-to-all(bf16[16,1280,128]{2,1,0:T(8,128)(2,1)} %place_packed.5), channel_id=1, replica_groups=mesh['site'=8,'sec'=16] {'sec'}, dimensions={0} | all-to-all | bytes 10485760 | tf_op jit(solution)/shard_map/all_to_all | solution.py:349
  536.8 11.8 %products_and_gram.5 = (f32[2,512,512]{2,1,0:T(8,128)}, bf16[8,512,512]{2,1,0:T(8,128)(2,1)}) custom-call(s32[8]{0:T(128)} %reshape.57.source_ref, bf16[16,512,512]{2,1,0:T(8,128)(2,1)} %all-to-all-done.tensor_ref, bf16[16,1280,128]{2,1,0:T(8,128)(2,1)} %all_to_all.21.factor_ref), custom_call_target="tpu_custom_call" | custom-call | tf_op jit(solution)/shard_map/products_and_gram/pallas_call | solution.py:138
  548.6 65.6 %factorize_last.1 = (f32[2,512,512]{2,1,0:T(8,128)}, bf16[2,512,512]{2,1,0:T(8,128)(2,1)}, bf16[2,512,512]{2,1,0:T(8,128)(2,1)}) custom-call(s32[2]{0:T(128)} %dynamic-slice_bitcast_fusion.1.width_ref, f32[2,512,512]{2,1,0:T(8,128)} %get-tuple-element.8.gram_ref), custom_call_target="tpu_custom_call" | custom-call | tf_op jit(solution)/shard_map/factorize_last/pallas_call | solution.py:297
  614.3 10.8 %isometries.1 = f32[8,512,512]{2,1,0:T(8,128)} custom-call(bf16[8,512,512]{2,1,0:T(8,128)(2,1)} %get-tuple-element.7.product_ref, bf16[2,512,512]{2,1,0:T(8,128)(2,1)} %get-tuple-element.9.high_ref, bf16[2,512,512]{2,1,0:T(8,128)(2,1)} %get-tuple-element.10.low_ref), custom_call_target="tpu_custom_call" | custom-call | tf_op jit(solution)/shard_map/isometries/pallas_call | solution.py:315
  (16 shorter events, 1.8 us)
Async XLA Ops:
  0.6 0.7 copy-start
  9.8 86.4 %all-to-all-start.1 = ((bf16[16,1280,128]{2,1,0:T(8,128)(2,1)}), bf16[16,1280,128]{2,1,0:T(8,128)(2,1)}, u32[]{:S(2)}, u32[]{:S(2)}) async-start(bf16[16,1280,128]{2,1,0:T(8,128)(2,1)} %place_packed.3), calls=%async_computation.1 | async-start | bytes 10485760 | tf_op jit(solution)/shard_map/all_to_all | solution.py:349
  96.3 127.4 %all-to-all-start = ((bf16[16,512,512]{2,1,0:T(8,128)(2,1)}), bf16[16,512,512]{2,1,0:T(8,128)(2,1)}, u32[]{:S(2)}, u32[]{:S(2)}) async-start(bf16[16,512,512]{2,1,0:T(8,128)(2,1)} %place_tensors.1), calls=%async_computation | async-start | bytes 16777216 | tf_op jit(solution)/shard_map/all_to_all | solution.py:349
  296.5 11.4 %collective-permute-start = (bf16[2,1280,128]{2,1,0:T(8,128)(2,1)}, bf16[2,1280,128]{2,1,0:T(8,128)(2,1)S(1)}, u32[]{:S(2)}, u32[]{:S(2)}) collective-permute-start(bf16[2,1280,128]{2,1,0:T(8,128)(2,1)} %factorize.2), channel_id=1, source_target_pairs={{0,16},{16,32},{32,48},{48,64},{64,80},{80,96},{96,112},{112,0},{1... | collective-permute-start | bytes 1966088 | tf_op jit(solution)/shard_map/ppermute | solution.py:25
  307.9 0.8 copy-start.3
  453.1 11.4 %collective-permute-start.1 = (bf16[2,1280,128]{2,1,0:T(8,128)(2,1)}, bf16[2,1280,128]{2,1,0:T(8,128)(2,1)S(1)}, u32[]{:S(2)}, u32[]{:S(2)}) collective-permute-start(bf16[2,1280,128]{2,1,0:T(8,128)(2,1)} %factorize.3), channel_id=1, source_target_pairs={{0,16},{16,32},{32,48},{48,64},{64,80},{80,96},{96,112},{112,0},{1... | collective-permute-start | bytes 1966088 | tf_op jit(solution)/shard_map/ppermute | solution.py:25
  464.5 0.8 copy-start.2
  614.3 10.8 %copy-start.1 = (s32[8,32,4]{1,2,0:T(4,128)S(1)}, s32[8,32,4]{1,2,0:T(4,128)}, u32[]{:S(2)}) copy-start(s32[8,32,4]{1,2,0:T(4,128)} %param.7) | copy-start | bytes 12292

commit v2 on v1

--- a/solution.py
+++ b/solution.py
@@ -42,39 +42,42 @@
     return pieces
 
 
-def place_tensor_kernel(slot_ref, block_ref, out_ref):
-    out_ref[...] = block_ref[...]
-
-
-def place_tensors(blocks, slots, groups):
-    count, rows, columns = blocks.shape
-    return pl.pallas_call(
-        place_tensor_kernel,
-        out_shape=jax.ShapeDtypeStruct((groups, rows, columns), blocks.dtype),
-        grid_spec=pltpu.PrefetchScalarGridSpec(
-            num_scalar_prefetch=1,
-            grid=(count,),
-            in_specs=[pl.BlockSpec((1, rows, columns), lambda g, slot: (g, 0, 0))],
-            out_specs=pl.BlockSpec((1, rows, columns), lambda g, slot: (slot[g], 0, 0)),
-        ),
-        name="place_tensors",
-    )(slots, blocks)
-
-
-def place_packed(packed, slots, groups, phys_count):
-    _, rows, columns = packed.shape
+def place_kernel(unique, count, slot_ref, block_ref, out_ref, held, read_sem, write_sem):
+    reads = [
+        pltpu.make_async_copy(block_ref.at[u], held.at[u], read_sem.at[u]) for u in range(unique)
+    ]
+    for read in reads:
+        read.start()
+    writes = []
+    share = count // unique
+    for u in range(unique):
+        reads[u].wait()
+        for g in range(u * share, (u + 1) * share):
+            write = pltpu.make_async_copy(held.at[u], out_ref.at[slot_ref[g]], write_sem.at[g])
+            write.start()
+            writes.append(write)
+    for write in writes:
+        write.wait()
+
+
+def place(blocks, slots, groups):
+    unique, rows, columns = blocks.shape
     count = slots.shape[0]
     return pl.pallas_call(
-        place_tensor_kernel,
-        out_shape=jax.ShapeDtypeStruct((groups, rows, columns), packed.dtype),
-        grid_spec=pltpu.PrefetchScalarGridSpec(
-            num_scalar_prefetch=1,
-            grid=(count,),
-            in_specs=[pl.BlockSpec((1, rows, columns), lambda g, slot: (g // phys_count, 0, 0))],
-            out_specs=pl.BlockSpec((1, rows, columns), lambda g, slot: (slot[g], 0, 0)),
-        ),
-        name="place_packed",
-    )(slots, packed)
+        functools.partial(place_kernel, unique, count),
+        out_shape=jax.ShapeDtypeStruct((groups, rows, columns), blocks.dtype),
+        in_specs=[
+            pl.BlockSpec(memory_space=pltpu.SMEM),
+            pl.BlockSpec(memory_space=pl.ANY),
+        ],
+        out_specs=pl.BlockSpec(memory_space=pl.ANY),
+        scratch_shapes=[
+            pltpu.VMEM(blocks.shape, blocks.dtype),
+            pltpu.SemaphoreType.DMA((unique,)),
+            pltpu.SemaphoreType.DMA((count,)),
+        ],
+        name="place",
+    )(slots, blocks)
 
 
 def pack_kernel(tiles, factor_ref, out_ref):
@@ -96,7 +99,7 @@
     )(factors)
 
 
-def product_kernel(tiles, phys_count, keep, source_ref, tensor_ref, factor_ref, gram_ref, *rest):
+def product_kernel(tiles, phys_count, source_ref, left_ref, tensor_ref, factor_ref, gram_ref, *rest):
     starts, _ = packed_starts(tiles)
     step = pl.program_id(0)
     product_ref = rest[0]
@@ -110,90 +113,124 @@
         )
         part = contract(row, tensor_ref[0, k * TILE :, :], 1, 0)
         product_ref[0, k * TILE : (k + 1) * TILE, :] = part.astype(BF16)
-    product = product_ref[0]
-    gram = contract(product, product, 0, 0)
-
-    @pl.when(step % phys_count == 0)
-    def _():
-        gram_ref[0] = gram
-
-    @pl.when(step % phys_count != 0)
-    def _():
-        gram_ref[0] += gram
-
-
-def products_and_gram(tensor_slots, factor_slots, sources, sec_local, phys_count, keep):
+    first = step % phys_count == 0
+    for k in range(tiles):
+        here = slice(k * TILE, (k + 1) * TILE)
+        part = contract(product_ref[0, :, here], product_ref[0, :, k * TILE :], 0, 0)
+
+        @pl.when(first)
+        def _(here=here, k=k, part=part):
+            gram_ref[0, here, k * TILE :] = part
+
+        @pl.when(jnp.logical_not(first))
+        def _(here=here, k=k, part=part):
+            gram_ref[0, here, k * TILE :] += part
+
+
+def products_and_gram(tensor_slots, factor_slots, sources, lefts, sec_local, phys_count, keep):
     _, size, _ = tensor_slots.shape
     _, packed_rows, _ = factor_slots.shape
     tiles = size // TILE
     count = sec_local * phys_count
     out_shape = [jax.ShapeDtypeStruct((sec_local, size, size), F32)]
-    out_specs = [pl.BlockSpec((1, size, size), lambda g, source: (g // phys_count, 0, 0))]
+    out_specs = [pl.BlockSpec((1, size, size), lambda g, source, left: (g // phys_count, 0, 0))]
     scratch = []
     if keep:
         out_shape.append(jax.ShapeDtypeStruct((count, size, size), BF16))
-        out_specs.append(pl.BlockSpec((1, size, size), lambda g, source: (g, 0, 0)))
+        out_specs.append(pl.BlockSpec((1, size, size), lambda g, source, left: (g, 0, 0)))
     else:
         scratch.append(pltpu.VMEM((1, size, size), BF16))
     return pl.pallas_call(
-        functools.partial(product_kernel, tiles, phys_count, keep),
+        functools.partial(product_kernel, tiles, phys_count),
         out_shape=out_shape,
         grid_spec=pltpu.PrefetchScalarGridSpec(
-            num_scalar_prefetch=1,
+            num_scalar_prefetch=2,
             grid=(count,),
             in_specs=[
-                pl.BlockSpec((1, size, size), lambda g, source: (source[g], 0, 0)),
-                pl.BlockSpec((1, packed_rows, TILE), lambda g, source: (source[g], 0, 0)),
+                pl.BlockSpec((1, size, size), lambda g, source, left: (source[g], 0, 0)),
+                pl.BlockSpec((1, packed_rows, TILE), lambda g, source, left: (left[g], 0, 0)),
             ],
             out_specs=out_specs,
             scratch_shapes=scratch,
         ),
         name="products_and_gram",
-    )(sources, tensor_slots, factor_slots)
+    )(sources, lefts, tensor_slots, factor_slots)
+
+
+def factor_group(rows8, j, lane, sub):
+    full = (8, TILE)
+    rows = [jnp.broadcast_to(rows8[t : t + 1, :], full) for t in range(8)]
+    units = [jnp.where(lane == j + t, 1.0, 0.0) for t in range(8)]
+    columns = [jnp.broadcast_to(rows8[:, j + u : j + u + 1], full) for u in range(8)]
+    block = [
+        [jnp.broadcast_to(columns[u][t : t + 1, :], full) if u >= t else None for u in range(8)]
+        for t in range(8)
+    ]
+    inverse, lower = [], {}
+    for t in range(8):
+        inverse.append(1.0 / block[t][t])
+        for u in range(t + 1, 8):
+            lower[u, t] = block[t][u] * inverse[t]
+        for u in range(t + 1, 8):
+            for v in range(u, 8):
+                block[u][v] = block[u][v] - lower[u, t] * block[t][v]
+    for t in range(8):
+        for v in range(t):
+            rows[t] = rows[t] - lower[t, v] * rows[v]
+            units[t] = units[t] - lower[t, v] * units[v]
+    upper = jnp.zeros(full, F32)
+    unit = jnp.zeros(full, F32)
+    for t in range(8):
+        root = lax.rsqrt(block[t][t])
+        upper = jnp.where(sub == t, rows[t] * root, upper)
+        unit = jnp.where(sub == t, units[t] * root, unit)
+    reduced = [rows[t] * inverse[t] for t in range(8)]
+    for t in range(7, -1, -1):
+        for v in range(t + 1, 8):
+            reduced[t] = reduced[t] - lower[v, t] * reduced[v]
+    return upper, unit, reduced
 
 
 def factor_tile(stacks):
-    done = [[] for _ in stacks]
-    groups = TILE // 8
+    groups, wide = TILE // 8, 4
+    lane = lax.broadcasted_iota(jnp.int32, (8, TILE), 1)
+    sub = lax.broadcasted_iota(jnp.int32, (8, TILE), 0)
+    uppers, units = [[] for _ in stacks], [[] for _ in stacks]
     for group in range(groups):
-        rows = [[] for _ in stacks]
-        for r in range(8):
-            j = group * 8 + r
+        j = group * 8
+        end = (group // wide + 1) * wide
+        for s, stack in enumerate(stacks):
+            upper, unit, reduced = factor_group(stack[group], j, lane, sub)
+            uppers[s].append(upper)
+            units[s].append(unit)
+            for i in range(group + 1, end):
+                total = None
+                for t in range(8):
+                    term = jnp.broadcast_to(stack[i][:, j + t : j + t + 1], (8, TILE)) * reduced[t]
+                    total = term if total is None else total + term
+                stack[i] = stack[i] - total
+        if end == group + 1 and end < groups:
             for s, stack in enumerate(stacks):
-                row = stack[group][r : r + 1, :]
-                pivot = jnp.broadcast_to(row[:, j : j + 1], (1, TILE))
-                rows[s].append(row * lax.rsqrt(pivot))
-                if j < TILE - 1:
-                    inverse = jnp.broadcast_to(1.0 / pivot, (8, TILE))
-                    wide = jnp.broadcast_to(row, (8, TILE))
-                    for i in range(group if r < 7 else group + 1, groups):
-                        column = jnp.broadcast_to(stack[i][:, j : j + 1], (8, TILE))
-                        stack[i] = stack[i] - column * wide * inverse
-        for s in range(len(stacks)):
-            done[s].append(jnp.concatenate(rows[s], axis=0))
-    return done
-
-
-def invert_tiles(uppers, row_id, column_id):
-    inverses = []
-    for upper in uppers:
-        diagonal = jnp.sum(jnp.where(row_id == column_id, upper, 0.0), axis=0, keepdims=True)
-        inverses.append(jnp.where(row_id == column_id, 1.0 / diagonal, 0.0))
-    span = 1
+                done = jnp.concatenate(uppers[s][end - wide :], axis=0)
+                update = contract(done, done, 0, 0, HIGHEST)
+                for i in range(end, groups):
+                    stack[i] = stack[i] - update[8 * i : 8 * i + 8]
+    return uppers, units
+
+
+def invert_tiles(uppers, units, row_id, column_id):
+    span = 8
     while span < TILE:
         pair = (row_id // (2 * span) == column_id // (2 * span)) & (
             row_id // span != column_id // span
         )
         inner = [
-            contract(jnp.where(pair, upper, 0.0), inverse, 1, 0, HIGHEST)
-            for upper, inverse in zip(uppers, inverses)
+            contract(unit, jnp.where(pair, upper, 0.0), 1, 1, HIGHEST)
+            for upper, unit in zip(uppers, units)
         ]
-        inverses = [
-            inverse - contract(inverse, part, 1, 0, HIGHEST)
-            for inverse, part in zip(inverses, inner)
-        ]
+        units = [unit - contract(part, unit, 1, 0, HIGHEST) for unit, part in zip(units, inner)]
         span *= 2
-    return inverses
+    return units
 
 
 def factor_kernel(count, tiles, final, scale, width_ref, gram_ref, *refs):
@@ -225,11 +262,13 @@
                     for i in range(TILE // 8)
                 ]
             )
+        upper_rows, unit_rows = factor_tile(stacks)
         uppers = [
             jnp.where(row_id <= column_id, jnp.concatenate(rows, axis=0), 0.0)
-            for rows in factor_tile(stacks)
+            for rows in upper_rows
         ]
-        inverses = invert_tiles(uppers, row_id, column_id)
+        units = [jnp.concatenate(rows, axis=0) for rows in unit_rows]
+        inverses = invert_tiles(uppers, units, row_id, column_id)
         for s in range(count):
             diag_inverse[s, pl.ds(first, TILE), :] = inverses[s]
         for k in range(tiles):
@@ -245,7 +284,7 @@
                         packed_ref[s, at : at + TILE, :] = uppers[s].astype(BF16)
                     if k + 1 == tiles:
                         continue
-                    panel = contract(inverses[s], work[s, lo:hi, hi:], 0, 0, HIGHEST)
+                    panel = contract(inverses[s], work[s, lo:hi, hi:], 1, 0, HIGHEST)
                     for q in range(k + 1, tiles):
                         left = (q - k - 1) * TILE
                         piece = panel[:, left : left + TILE]
@@ -267,7 +306,7 @@
             full[...] = jnp.zeros((size, size), F32)
             for k in range(tiles):
                 lo, hi = k * TILE, (k + 1) * TILE
-                full[lo:hi, lo:hi] = diag_inverse[s, lo:hi, :]
+                full[lo:hi, lo:hi] = jnp.transpose(diag_inverse[s, lo:hi, :])
             span = TILE
             while span < size:
                 for lo in range(0, size, 2 * span):
@@ -305,8 +344,13 @@
 
 
 def isometry_kernel(product_ref, high_ref, low_ref, out_ref):
-    product = product_ref[0]
-    out_ref[0] = contract(product, high_ref[0], 1, 0) + contract(product, low_ref[0], 1, 0)
+    size = product_ref.shape[1]
+    for lo in range(0, size, 2 * TILE):
+        hi = lo + 2 * TILE
+        left = product_ref[0, :, :hi]
+        out_ref[0, :, lo:hi] = contract(left, high_ref[0, :hi, lo:hi], 1, 0) + contract(
+            left, low_ref[0, :hi, lo:hi], 1, 0
+        )
 
 
 def isometries(products, high, low, phys_count):
@@ -342,24 +386,28 @@
     widths = lax.dynamic_slice_in_dim(next_widths, first, sec_local)
     slots = lax.dynamic_slice_in_dim(rows, first, sec_local).reshape(count) // sec_local
     wanted = rows[None] == (first + jnp.arange(sec_local, dtype=jnp.int32))[:, None, None]
-    owner = jnp.arange(rows.shape[0], dtype=jnp.int32)[None, :, None] // sec_local
-    sources = jnp.sum(jnp.where(wanted, owner, 0), axis=1).reshape(count)
+    order = jnp.arange(rows.shape[0], dtype=jnp.int32)[None, :, None]
+    lefts = jnp.sum(jnp.where(wanted, order, 0), axis=1).reshape(count)
+    sources = lefts // sec_local
 
     def exchange(slotted):
         return lax.all_to_all(slotted, "sec", split_axis=0, concat_axis=0, tiled=True)
 
-    tensor_slots = exchange(place_tensors(blocks.reshape(count, size, size), slots, groups))
     packed = pack_factors(factors[0])
+    factor_slots = lax.all_gather(packed, "sec", axis=0, tiled=True)
+    tensor_slots = exchange(place(blocks.reshape(count, size, size), slots, groups))
     scale = math.sqrt(phys_count * size)
+    which = lefts
     for round_index in range(ROUNDS):
         final = round_index + 1 == ROUNDS
-        factor_slots = exchange(place_packed(packed, slots, groups, phys_count))
         gram, *products = products_and_gram(
-            tensor_slots, factor_slots, sources, sec_local, phys_count, final
+            tensor_slots, factor_slots, sources, which, sec_local, phys_count, final
         )
         outs = factorize(gram, widths, final, scale)
         if not final:
             packed = from_behind(outs[0], "site", 1)
+            factor_slots = exchange(place(packed, slots, groups))
+            which = sources
     upper, high, low = outs
     isometry = isometries(products[0], high, low, phys_count)
     return isometry.reshape(1, sec_local, phys_count, size, size), upper[None]

time: 636 us -> 535 us (0.84); the launches traced: 626 us -> 534 us
  Pallas kernels: 259 us -> 179 us
  waiting for transfers between devices: 214 us -> 191 us
  between operations: 1.16 us -> 14.1 us
    pallas_call x3, Pallas kernels: 189 us -> 112 us  [factorize(): pl.pallas_call(functools.partial(factor_kernel, count, tiles, final, scal...]
    all_to_all x2 -> x1, waiting for transfers between devices: 191 us -> 151 us  [exchange(): lax.all_to_all(slotted, 'sec', split_axis=0, concat_axis=0, tiled=True)]
    all_gather x0 -> x1, waiting for transfers between devices: none -> 17.9 us  [body(): factor_slots = lax.all_gather(packed, 'sec', axis=0, tiled=True)]
    all_to_all x2 -> x1, starting transfers between devices: 13.5 us -> 8.22 us  [exchange(): lax.all_to_all(slotted, 'sec', split_axis=0, concat_axis=0, tiled=True)]
    pallas_call x7 -> x6, Pallas kernels: 56.9 us -> 54.3 us  [the longest x3 43.7 us: products_and_gram(): pl.pallas_call(functools.partial(product_kernel, tiles, phys_count), out_...]
  transfers between devices with their start and end apart: 4 -> 4, of which waited for: 4 -> 4; matrix products, arithmetic and copies ran while one was open for 0% -> 1% of each run, Pallas kernels for 1% -> 1%
where the time goes in v2:
time: 535 us; the launch traced here: 534 us
  waiting for transfers between devices  191 us (36%)
  Pallas kernels  179 us (33%)
  blocking collectives  137 us (26%)
  between operations  14.1 us (3%)
  starting transfers between devices  8.27 us (2%)
    all_to_all x1, waiting for transfers between devices, exchange(): lax.all_to_all(slotted, 'sec', split_axis=0, concat_axis=0, tiled=True)  151 us
    all_to_all x2, blocking collectives, exchange(): lax.all_to_all(slotted, 'sec', split_axis=0, concat_axis=0, tiled=True)  137 us
    pallas_call x3, Pallas kernels, factorize(): pl.pallas_call(functools.partial(factor_kernel, count, tiles, final, scal...  112 us
    pallas_call x3, Pallas kernels, products_and_gram(): pl.pallas_call(functools.partial(product_kernel, tiles, phys_count), out_...  43.7 us
    ppermute x2, waiting for transfers between devices, from_behind(): lax.ppermute(shard, axis, [(i, (i + by) % size) for i in range(size)])  22.9 us
    all_gather x1, waiting for transfers between devices, body(): factor_slots = lax.all_gather(packed, 'sec', axis=0, tiled=True)  17.9 us
  transfers between devices with their start and end apart: 4, of which 4 were waited for; matrix products, arithmetic and copies ran while one was open for 1% of the time, Pallas kernels for 1%

profile of v2, /device:TPU:0, one launch (start us, length us, event | category | flops | bytes accessed | tf_op | source)
XLA Modules:
  0.0 534.2 jit_solution(12065284611838176559)
XLA Ops:
  7.2 2.3 pack_factors.1
  9.9 0.6 and_select_fusion.slot_ref
  10.4 4.2 place.3
  14.7 8.2 %all-to-all-start = ((bf16[16,512,512]{2,1,0:T(8,128)(2,1)}), bf16[16,512,512]{2,1,0:T(8,128)(2,1)}, u32[]{:S(2)}, u32[]{:S(2)}) async-start(bf16[16,512,512]{2,1,0:T(8,128)(2,1)} %place.3), calls=%async_computation | async-start | bytes 16777216 | tf_op jit(solution)/shard_map/all_to_all | solution.py:394
  23.0 0.2 select_reduce_fusion
  23.3 1.3 dynamic-slice_bitcast_fusion.1.width_ref
  24.5 0.6 and_select_fusion.1.source_ref.left_ref
  25.1 150.5 %all-to-all-done.tensor_ref = bf16[16,512,512]{2,1,0:T(8,128)(2,1)} async-done(((bf16[16,512,512]{2,1,0:T(8,128)(2,1)}), bf16[16,512,512]{2,1,0:T(8,128)(2,1)}, u32[]{:S(2)}, u32[]{:S(2)}) %all-to-all-start) | async-done | bytes 8388640 | tf_op jit(solution)/shard_map/all_to_all | solution.py:394
  175.6 17.9 %all-gather.2.cloned.1.call-done.factor_ref = bf16[32,1280,128]{2,1,0:T(8,128)(2,1)} async-done(((bf16[2,1280,128]{2,1,0:T(8,128)(2,1)}), bf16[32,1280,128]{2,1,0:T(8,128)(2,1)}) %all-gather.2.cloned.1.call-update) | async-done | bytes 10485776 | tf_op jit(solution)/shard_map/all_gather | solution.py:397
  193.5 14.4 %products_and_gram.3.gram_ref = f32[2,512,512]{2,1,0:T(8,128)} custom-call(s32[8]{0:T(128)} %and_select_fusion.1.source_ref.left_ref, s32[8]{0:T(128)} %copy-done.4, bf16[16,512,512]{2,1,0:T(8,128)(2,1)} %all-to-all-done.tensor_ref, bf16[32,1280,128]{2,1,0:T(8,128)(2,1)} %all-gather.2.cloned.1.call-done.factor_ref), custom_call_target="tpu_custom_call" | custom-call | tf_op jit(solution)/shard_map/products_and_gram/pallas_call | solution.py:143
  207.9 36.1 %factorize.2 = bf16[2,1280,128]{2,1,0:T(8,128)(2,1)} custom-call(s32[2]{0:T(128)} %dynamic-slice_bitcast_fusion.1.width_ref, f32[2,512,512]{2,1,0:T(8,128)} %products_and_gram.3.gram_ref), custom_call_target="tpu_custom_call" | custom-call | tf_op jit(solution)/shard_map/factorize/pallas_call | solution.py:336
  244.0 11.4 %collective-permute-done.block_ref = bf16[2,1280,128]{2,1,0:T(8,128)(2,1)S(1)} collective-permute-done((bf16[2,1280,128]{2,1,0:T(8,128)(2,1)}, bf16[2,1280,128]{2,1,0:T(8,128)(2,1)S(1)}, u32[]{:S(2)}, u32[]{:S(2)}) %collective-permute-start) | collective-permute-done | bytes 655392 | tf_op jit(solution)/shard_map/ppermute | solution.py:25
  255.4 0.8 copy-done.3
  256.3 3.2 place.4
  259.5 70.9 %all_to_all.15.factor_ref = bf16[16,1280,128]{2,1,0:T(8,128)(2,1)} all-to-all(bf16[16,1280,128]{2,1,0:T(8,128)(2,1)} %place.4), channel_id=1, replica_groups=mesh['site'=8,'sec'=16] {'sec'}, dimensions={0} | all-to-all | bytes 10485760 | tf_op jit(solution)/shard_map/all_to_all | solution.py:394
  330.4 14.4 %products_and_gram.4.gram_ref = f32[2,512,512]{2,1,0:T(8,128)} custom-call(s32[8]{0:T(128)} %and_select_fusion.1.source_ref.left_ref, s32[8]{0:T(128)} %and_select_fusion.1.source_ref.left_ref, bf16[16,512,512]{2,1,0:T(8,128)(2,1)} %all-to-all-done.tensor_ref, bf16[16,1280,128]{2,1,0:T(8,128)(2,1)} %all_to_all.15.factor_ref), custom_call_target="tpu_custom_call" | custom-call | tf_op jit(solution)/shard_map/products_and_gram/pallas_call | solution.py:143
  344.8 36.1 %factorize.3 = bf16[2,1280,128]{2,1,0:T(8,128)(2,1)} custom-call(s32[2]{0:T(128)} %dynamic-slice_bitcast_fusion.1.width_ref, f32[2,512,512]{2,1,0:T(8,128)} %products_and_gram.4.gram_ref), custom_call_target="tpu_custom_call" | custom-call | tf_op jit(solution)/shard_map/factorize/pallas_call | solution.py:336
  380.9 11.4 %collective-permute-done.1.block_ref = bf16[2,1280,128]{2,1,0:T(8,128)(2,1)S(1)} collective-permute-done((bf16[2,1280,128]{2,1,0:T(8,128)(2,1)}, bf16[2,1280,128]{2,1,0:T(8,128)(2,1)S(1)}, u32[]{:S(2)}, u32[]{:S(2)}) %collective-permute-start.1) | collective-permute-done | bytes 655392 | tf_op jit(solution)/shard_map/ppermute | solution.py:25
  392.3 0.8 copy-done.2
  393.1 3.2 place.5
  396.3 66.1 %all_to_all.16.factor_ref = bf16[16,1280,128]{2,1,0:T(8,128)(2,1)} all-to-all(bf16[16,1280,128]{2,1,0:T(8,128)(2,1)} %place.5), channel_id=1, replica_groups=mesh['site'=8,'sec'=16] {'sec'}, dimensions={0} | all-to-all | bytes 10485760 | tf_op jit(solution)/shard_map/all_to_all | solution.py:394
  462.4 14.9 %products_and_gram.5 = (f32[2,512,512]{2,1,0:T(8,128)}, bf16[8,512,512]{2,1,0:T(8,128)(2,1)}) custom-call(s32[8]{0:T(128)} %and_select_fusion.1.source_ref.left_ref, s32[8]{0:T(128)} %and_select_fusion.1.source_ref.left_ref, bf16[16,512,512]{2,1,0:T(8,128)(2,1)} %all-to-all-done.tensor_ref, bf16[16,1280,128]{2,1,0:T(8,128)(2,1)} %all_to_all.16.factor_ref), custom_call_target="tpu_custom_call" | custom-call | tf_op jit(solution)/shard_map/products_and_gram/pallas_call | solution.py:143
  477.3 39.8 %factorize_last.1 = (f32[2,512,512]{2,1,0:T(8,128)}, bf16[2,512,512]{2,1,0:T(8,128)(2,1)}, bf16[2,512,512]{2,1,0:T(8,128)(2,1)}) custom-call(s32[2]{0:T(128)} %dynamic-slice_bitcast_fusion.1.width_ref, f32[2,512,512]{2,1,0:T(8,128)} %get-tuple-element.8.gram_ref), custom_call_target="tpu_custom_call" | custom-call | tf_op jit(solution)/shard_map/factorize_last/pallas_call | solution.py:336
  517.1 10.3 %isometries.1 = f32[8,512,512]{2,1,0:T(8,128)} custom-call(bf16[8,512,512]{2,1,0:T(8,128)(2,1)} %get-tuple-element.7.product_ref, bf16[2,512,512]{2,1,0:T(8,128)(2,1)} %get-tuple-element.9.high_ref, bf16[2,512,512]{2,1,0:T(8,128)(2,1)} %get-tuple-element.10.low_ref), custom_call_target="tpu_custom_call" | custom-call | tf_op jit(solution)/shard_map/isometries/pallas_call | solution.py:359
  (18 shorter events, 0.4 us)
Async XLA Ops:
  7.2 2.4 copy-start
  7.2 186.3 %all-gather.2.cloned.1.call-start = ((), (), s32[]{:S(2)}) async-start(), calls=%async_computation.3 | async-start | bytes 11141120 | tf_op jit(solution)/shard_map/all_gather | solution.py:397
  14.7 161.0 %all-to-all-start = ((bf16[16,512,512]{2,1,0:T(8,128)(2,1)}), bf16[16,512,512]{2,1,0:T(8,128)(2,1)}, u32[]{:S(2)}, u32[]{:S(2)}) async-start(bf16[16,512,512]{2,1,0:T(8,128)(2,1)} %place.3), calls=%async_computation | async-start | bytes 16777216 | tf_op jit(solution)/shard_map/all_to_all | solution.py:394
  23.3 170.3 %copy-start.4 = (s32[8]{0:T(128)}, s32[8]{0:T(128)S(1)}, u32[]{:S(2)}) copy-start(s32[8]{0:T(128)S(1)} %reshape.20.left_ref) | copy-start | bytes 100
  244.0 11.4 %collective-permute-start = (bf16[2,1280,128]{2,1,0:T(8,128)(2,1)}, bf16[2,1280,128]{2,1,0:T(8,128)(2,1)S(1)}, u32[]{:S(2)}, u32[]{:S(2)}) collective-permute-start(bf16[2,1280,128]{2,1,0:T(8,128)(2,1)} %factorize.2), channel_id=1, source_target_pairs={{0,16},{16,32},{32,48},{48,64},{64,80},{80,96},{96,112},{112,0},{1... | collective-permute-start | bytes 1966088 | tf_op jit(solution)/shard_map/ppermute | solution.py:25
  255.4 0.8 copy-start.3
  380.9 11.4 %collective-permute-start.1 = (bf16[2,1280,128]{2,1,0:T(8,128)(2,1)}, bf16[2,1280,128]{2,1,0:T(8,128)(2,1)S(1)}, u32[]{:S(2)}, u32[]{:S(2)}) collective-permute-start(bf16[2,1280,128]{2,1,0:T(8,128)(2,1)} %factorize.3), channel_id=1, source_target_pairs={{0,16},{16,32},{32,48},{48,64},{64,80},{80,96},{96,112},{112,0},{1... | collective-permute-start | bytes 1966088 | tf_op jit(solution)/shard_map/ppermute | solution.py:25
  392.3 0.8 copy-start.2
  517.1 10.3 %copy-start.1 = (s32[8,32,4]{1,2,0:T(4,128)S(1)}, s32[8,32,4]{1,2,0:T(4,128)}, u32[]{:S(2)}) copy-start(s32[8,32,4]{1,2,0:T(4,128)} %param.7) | copy-start | bytes 12292
Sparse Core Ops, SparseCore 0:
  10.7 182.7 all-gather.1

commit v3 on v2

v3 whole, which is shorter than its diff:
```python
import functools
import math

import jax
import jax.numpy as jnp
from jax import lax
from jax.experimental import pallas as pl
from jax.experimental.pallas import tpu as pltpu
from jax.sharding import PartitionSpec as P

ROUNDS = 3
F32 = jnp.float32
BF16 = jnp.bfloat16
TILE = 128
HIGHEST = lax.Precision.HIGHEST


def contract(left, right, left_dim, right_dim, precision=None):
    dims = (((left_dim,), (right_dim,)), ((), ()))
    return lax.dot_general(left, right, dims, precision=precision, preferred_element_type=F32)


def from_behind(shard, axis, by):
    size = lax.axis_size(axis)
    return lax.ppermute(shard, axis, [(i, (i + by) % size) for i in range(size)])


class Packing:
    SPARE = 16

    def __init__(self, tiles):
        self.tiles = tiles
        self.row = {}
        at = 0
        for k in range(tiles):
            for q in range(k + 1, tiles):
                self.row[k, q] = at
                at += TILE
        for pair in range(tiles // 2):
            self.row[pair] = at
            at += TILE
        self.diagonals = at
        self.rows = at + self.SPARE


def ids():
    row_id = lax.broadcasted_iota(jnp.int32, (TILE, TILE), 0)
    column_id = lax.broadcasted_iota(jnp.int32, (TILE, TILE), 1)
    return row_id, column_id


def pack_pair(even, odd, row_id, column_id):
    return jnp.where(row_id <= column_id, even, jnp.transpose(odd)).astype(BF16)


def pack_diagonals(odds, row_id, column_id):
    spare = lax.broadcasted_iota(jnp.int32, (Packing.SPARE, TILE), 0)
    rows = jnp.zeros((Packing.SPARE, TILE), F32)
    for pair, odd in enumerate(odds):
        diagonal = jnp.sum(jnp.where(row_id == column_id, odd, 0.0), axis=0, keepdims=True)
        rows = jnp.where(spare == pair, jnp.broadcast_to(diagonal, rows.shape), rows)
    return rows.astype(BF16)


def unpack_diagonals(packing, held, row_id, column_id):
    diagonals = held[packing.diagonals : packing.diagonals + Packing.SPARE, :].astype(F32)
    tiles = []
    for pair in range(packing.tiles // 2):
        at = packing.row[pair]
        both = held[at : at + TILE, :].astype(F32)
        diagonal = jnp.broadcast_to(diagonals[pair : pair + 1, :], both.shape)
        odd = jnp.where(
            row_id > column_id, both, jnp.where(row_id == column_id, diagonal, 0.0)
        )
        tiles.append(jnp.where(row_id <= column_id, both, 0.0).astype(BF16))
        tiles.append(jnp.transpose(odd).astype(BF16))
    return tiles


def start_all(copies):
    for copy in copies:
        copy.start()
    return copies


def wait_all(copies):
    for copy in copies:
        copy.wait()


def place_first_kernel(
    unique, count, tiles, slot_ref, factor_ref, block_ref, out_ref,
    square, held, packed, factor_sem, read_sem, write_sem, packed_sem,
):
    packing = Packing(tiles)
    size = tiles * TILE
    row_id, column_id = ids()
    factor_reads = start_all(
        [pltpu.make_async_copy(factor_ref.at[u], square.at[u], factor_sem.at[u]) for u in range(unique)]
    )
    reads = start_all(
        [pltpu.make_async_copy(block_ref.at[g], held.at[g], read_sem.at[g]) for g in range(count)]
    )
    writes = []
    share = count // unique
    for u in range(unique):
        factor_reads[u].wait()
        tile = {}
        for k in range(tiles):
            for q in range(k, tiles):
                tile[k, q] = square[u, k * TILE : (k + 1) * TILE, q * TILE : (q + 1) * TILE]
                if q > k:
                    at = packing.row[k, q]
                    packed[u, at : at + TILE, :] = tile[k, q].astype(BF16)
        for pair in range(tiles // 2):
            at = packing.row[pair]
            even, odd = tile[2 * pair, 2 * pair], tile[2 * pair + 1, 2 * pair + 1]
            packed[u, at : at + TILE, :] = pack_pair(even, odd, row_id, column_id)
        odds = [tile[k, k] for k in range(1, tiles, 2)]
        packed[u, packing.diagonals :, :] = pack_diagonals(odds, row_id, column_id)
    for g in range(count):
        reads[g].wait()
        slot = slot_ref[g]
        for q in range(tiles):
            writes.append(
                pltpu.make_async_copy(
                    held.at[g, :, q * TILE : (q + 1) * TILE],
                    out_ref.at[slot, q * size : (q + 1) * size, :],
                    write_sem.at[g, q],
                )
            )
            writes[-1].start()
        writes.append(
            pltpu.make_async_copy(
                packed.at[g // share],
                out_ref.at[slot, tiles * size : tiles * size + packing.rows, :],
                packed_sem.at[g],
            )
        )
        writes[-1].start()
    wait_all(writes)


def place_first(blocks, factors, slots, groups):
    count, size, _ = blocks.shape
    unique = factors.shape[0]
    tiles = size // TILE
    packing = Packing(tiles)
    anywhere = pl.BlockSpec(memory_space=pl.ANY)
    return pl.pallas_call(
        functools.partial(place_first_kernel, unique, count, tiles),
        out_shape=jax.ShapeDtypeStruct((groups, tiles * size + packing.rows, TILE), BF16),
        in_specs=[pl.BlockSpec(memory_space=pltpu.SMEM), anywhere, anywhere],
        out_specs=anywhere,
        scratch_shapes=[
            pltpu.VMEM(factors.shape, F32),
            pltpu.VMEM(blocks.shape, BF16),
            pltpu.VMEM((unique, packing.rows, TILE), BF16),
            pltpu.SemaphoreType.DMA((unique,)),
            pltpu.SemaphoreType.DMA((count,)),
            pltpu.SemaphoreType.DMA((count, tiles)),
            pltpu.SemaphoreType.DMA((count,)),
        ],
        name="place_first",
    )(slots, factors, blocks)


def place_kernel(unique, count, slot_ref, block_ref, out_ref, write_sem):
    share = count // unique
    wait_all(
        start_all(
            [
                pltpu.make_async_copy(
                    block_ref.at[g // share], out_ref.at[slot_ref[g]], write_sem.at[g]
                )
                for g in range(count)
            ]
        )
    )


def place(blocks, slots, groups):
    unique, rows, columns = blocks.shape
    count = slots.shape[0]
    return pl.pallas_call(
        functools.partial(place_kernel, unique, count),
        out_shape=jax.ShapeDtypeStruct((groups, rows, columns), blocks.dtype),
        in_specs=[
            pl.BlockSpec(memory_space=pltpu.SMEM),
            pl.BlockSpec(memory_space=pltpu.VMEM),
        ],
        out_specs=pl.BlockSpec(memory_space=pl.ANY),
        scratch_shapes=[
            pltpu.SemaphoreType.DMA((count,)),
        ],
        name="place",
    )(slots, blocks)


def factor_group(rows8, j, lane, sub):
    full = (8, TILE)
    rows = [jnp.broadcast_to(rows8[t : t + 1, :], full) for t in range(8)]
    units = [jnp.where(lane == j + t, 1.0, 0.0) for t in range(8)]
    columns = [jnp.broadcast_to(rows8[:, j + u : j + u + 1], full) for u in range(8)]
    block = [
        [jnp.broadcast_to(columns[u][t : t + 1, :], full) if u >= t else None for u in range(8)]
        for t in range(8)
    ]
    inverse, lower = [], {}
    for t in range(8):
        inverse.append(1.0 / block[t][t])
        for u in range(t + 1, 8):
            lower[u, t] = block[t][u] * inverse[t]
        for u in range(t + 1, 8):
            for v in range(u, 8):
                block[u][v] = block[u][v] - lower[u, t] * block[t][v]
    for t in range(8):
        for v in range(t):
            rows[t] = rows[t] - lower[t, v] * rows[v]
            units[t] = units[t] - lower[t, v] * units[v]
    upper = jnp.zeros(full, F32)
    unit = jnp.zeros(full, F32)
    for t in range(8):
        root = lax.rsqrt(block[t][t])
        upper = jnp.where(sub == t, rows[t] * root, upper)
        unit = jnp.where(sub == t, units[t] * root, unit)
    reduced = [rows[t] * inverse[t] for t in range(8)]
    for t in range(7, -1, -1):
        for v in range(t + 1, 8):
            reduced[t] = reduced[t] - lower[v, t] * reduced[v]
    return upper, unit, reduced


def factor_tile(stacks):
    groups, wide = TILE // 8, 4
    lane = lax.broadcasted_iota(jnp.int32, (8, TILE), 1)
    sub = lax.broadcasted_iota(jnp.int32, (8, TILE), 0)
    uppers, units = [[] for _ in stacks], [[] for _ in stacks]
    for group in range(groups):
        j = group * 8
        end = (group // wide + 1) * wide
        for s, stack in enumerate(stacks):
            upper, unit, reduced = factor_group(stack[group], j, lane, sub)
            uppers[s].append(upper)
            units[s].append(unit)
            for i in range(group + 1, end):
                total = None
                for t in range(8):
                    term = jnp.broadcast_to(stack[i][:, j + t : j + t + 1], (8, TILE)) * reduced[t]
                    total = term if total is None else total + term
                stack[i] = stack[i] - total
        if end == group + 1 and end < groups:
            for s, stack in enumerate(stacks):
                done = jnp.concatenate(uppers[s][end - wide :], axis=0)
                update = contract(done, done, 0, 0, HIGHEST)
                for i in range(end, groups):
                    stack[i] = stack[i] - update[8 * i : 8 * i + 8]
    return uppers, units


def invert_tiles(uppers, units, row_id, column_id):
    span = 8
    while span < TILE:
        pair = (row_id // (2 * span) == column_id // (2 * span)) & (
            row_id // span != column_id // span
        )
        inner = [
            contract(unit, jnp.where(pair, upper, 0.0), 1, 1, HIGHEST)
            for upper, unit in zip(uppers, units)
        ]
        units = [unit - contract(part, unit, 1, 0, HIGHEST) for unit, part in zip(units, inner)]
        span *= 2
    return units


def round_kernel(sec_local, phys_count, tiles, shared, final, *refs):
    refs = list(refs)
    source_ref, width_ref, tensor_slots = refs[:3]
    factor_slots = tensor_slots if shared else refs[3]
    refs = refs[3 if shared else 4 :]
    outs, refs = refs[: 2 if final else 1], refs[2 if final else 1 :]
    tensors, factors, products, work, diag_inverse, tensor_sem, factor_sem = refs[:7]
    packing = Packing(tiles)
    size = tiles * TILE
    count = sec_local * phys_count
    row_id, column_id = ids()
    if final:
        isometry_ref, upper_out = outs
        upper_ref, full, staged, upper_sem, isometry_sem = refs[7:]
    else:
        packed_ref = outs[0]
    at_factor = tiles * size if shared else 0

    def tensor_copy(g, q):
        return pltpu.make_async_copy(
            tensor_slots.at[source_ref[g], q * size : (q + 1) * size, :],
            tensors.at[g, :, q * TILE : (q + 1) * TILE],
            tensor_sem.at[g, q],
        )

    def factor_copy(g):
        return pltpu.make_async_copy(
            factor_slots.at[source_ref[g], at_factor : at_factor + packing.rows, :],
            factors.at[g],
            factor_sem.at[g],
        )

    for g in range(count):
        factor_copy(g).start()
        for q in range(tiles):
            tensor_copy(g, q).start()

    def multiply(g, carry):
        factor_copy(g).wait()
        for q in range(tiles):
            tensor_copy(g, q).wait()
        held = factors.at[g]
        diagonal = unpack_diagonals(packing, held, row_id, column_id)
        for k in range(tiles):
            row = [diagonal[k]]
            for q in range(k + 1, tiles):
                at = packing.row[k, q]
                row.append(held[at : at + TILE, :])
            row = jnp.concatenate(row, axis=1) if len(row) > 1 else row[0]
            part = contract(row, tensors[g, k * TILE :, :], 1, 0)
            products[g, k * TILE : (k + 1) * TILE, :] = part.astype(BF16)
        return carry

    lax.fori_loop(0, count, multiply, 0)
    half = size // 2
    for s in range(sec_local):
        here = slice(s * phys_count, (s + 1) * phys_count)
        stacked = products[here].reshape(phys_count * size, size)
        work[s, :half, :] = contract(stacked[:, :half], stacked, 0, 0)
        work[s, half:, half:] = contract(stacked[:, half:], stacked[:, half:], 0, 0)
        for k in range(tiles):
            lo, hi = k * TILE, (k + 1) * TILE
            on = (row_id == column_id) & (row_id + lo >= width_ref[s])
            work[s, lo:hi, lo:hi] = work[s, lo:hi, lo:hi] + jnp.where(on, 1.0, 0.0)
        if final:
            upper_ref[s] = jnp.zeros((size, size), F32)

    def step(p, carry):
        first = pl.multiple_of(p * TILE, TILE)
        stacks = []
        for s in range(sec_local):
            stacks.append(
                [
                    work[s, pl.ds(pl.multiple_of(first + 8 * i, 8), 8), pl.ds(first, TILE)]
                    for i in range(TILE // 8)
                ]
            )
        upper_rows, unit_rows = factor_tile(stacks)
        uppers = [
            jnp.where(row_id <= column_id, jnp.concatenate(rows, axis=0), 0.0)
            for rows in upper_rows
        ]
        units = [jnp.concatenate(rows, axis=0) for rows in unit_rows]
        inverses = invert_tiles(uppers, units, row_id, column_id)
        if final:
            for s in range(sec_local):
                diag_inverse[s, pl.ds(first, TILE), :] = inverses[s]
        else:
            for s in range(sec_local):
                diag_inverse[s, pl.ds(first, TILE), :] = uppers[s]
        for k in range(tiles):

            @pl.when(p == k)
            def _(k=k):
                lo, hi = k * TILE, (k + 1) * TILE
                for s in range(sec_local):
                    if final:
                        upper_ref[s, lo:hi, lo:hi] = uppers[s]
                    if k + 1 == tiles:
                        continue
                    panel = contract(inverses[s], work[s, lo:hi, hi:], 1, 0, HIGHEST)
                    for q in range(k + 1, tiles):
                        left = (q - k - 1) * TILE
                        piece = panel[:, left : left + TILE]
                        if final:
                            upper_ref[s, lo:hi, q * TILE : (q + 1) * TILE] = piece
                        else:
                            at = packing.row[k, q]
                            packed_ref[s, at : at + TILE, :] = piece.astype(BF16)
                        here = slice(q * TILE, (q + 1) * TILE)
                        work[s, here, q * TILE :] = work[s, here, q * TILE :] - contract(
                            piece, panel[:, left:], 0, 0, HIGHEST
                        )

        return carry

    lax.fori_loop(0, tiles, step, 0)
    if not final:
        for s in range(sec_local):
            diagonal = [diag_inverse[s, k * TILE : (k + 1) * TILE, :] for k in range(tiles)]
            for pair in range(tiles // 2):
                at = packing.row[pair]
                packed_ref[s, at : at + TILE, :] = pack_pair(
                    diagonal[2 * pair], diagonal[2 * pair + 1], row_id, column_id
                )
            packed_ref[s, packing.diagonals :, :] = pack_diagonals(
                diagonal[1::2], row_id, column_id
            )
        return
    uppers_out = start_all(
        [
            pltpu.make_async_copy(upper_ref.at[s], upper_out.at[s], upper_sem.at[s])
            for s in range(sec_local)
        ]
    )
    scale = math.sqrt(phys_count * size)
    isometry_out = []
    for s in range(sec_local):
        inverse = full.at[s]
        for k in range(tiles):
            lo, hi = k * TILE, (k + 1) * TILE
            inverse[lo:hi, lo:hi] = jnp.transpose(diag_inverse[s, lo:hi, :])
            if k % 2 == 1:
                inverse[lo:hi, lo - TILE : lo] = jnp.zeros((TILE, TILE), F32)
        span = TILE
        while span < size:
            for lo in range(0, size, 2 * span):
                mid, hi = lo + span, lo + 2 * span
                inner = contract(
                    upper_ref[s, lo:mid, mid:hi], inverse[mid:hi, mid:hi], 1, 0, HIGHEST
                )
                inverse[lo:mid, mid:hi] = -contract(inverse[lo:mid, lo:mid], inner, 1, 0, HIGHEST)
                if span > TILE:
                    inverse[mid:hi, lo:mid] = jnp.zeros((span, span), F32)
            span *= 2
    for s in range(sec_local):
        scaled = full[s] * scale
        high = scaled.astype(BF16)
        low = (scaled - high.astype(F32)).astype(BF16)
        for p in range(phys_count):
            g = s * phys_count + p
            for lo in range(0, size, 2 * TILE):
                hi = lo + 2 * TILE
                left = products[g, :, :hi]
                staged[g, :, lo:hi] = contract(left, high[:hi, lo:hi], 1, 0) + contract(
                    left, low[:hi, lo:hi], 1, 0
                )
            isometry_out.append(
                pltpu.make_async_copy(staged.at[g], isometry_ref.at[g], isometry_sem.at[g])
            )
            isometry_out[-1].start()
    wait_all(uppers_out + isometry_out)


def run_round(sources, widths, tensor_slots, factor_slots, sec_local, phys_count, size, final):
    tiles = size // TILE
    packing = Packing(tiles)
    count = sec_local * phys_count
    anywhere = pl.BlockSpec(memory_space=pl.ANY)
    smem = pl.BlockSpec(memory_space=pltpu.SMEM)
    shared = factor_slots is None
    operands = [sources, widths, tensor_slots] + ([] if shared else [factor_slots])
    scratch = [
        pltpu.VMEM((count, size, size), BF16),
        pltpu.VMEM((count, packing.rows, TILE), BF16),
        pltpu.VMEM((count, size, size), BF16),
        pltpu.VMEM((sec_local, size, size), F32),
        pltpu.VMEM((sec_local, size, TILE), F32),
        pltpu.SemaphoreType.DMA((count, tiles)),
        pltpu.SemaphoreType.DMA((count,)),
    ]
    if final:
        out_shape = [
            jax.ShapeDtypeStruct((count, size, size), F32),
            jax.ShapeDtypeStruct((sec_local, size, size), F32),
        ]
        out_specs = [anywhere, anywhere]
        scratch += [
            pltpu.VMEM((sec_local, size, size), F32),
            pltpu.VMEM((sec_local, size, size), F32),
            pltpu.VMEM((count, size, size), F32),
            pltpu.SemaphoreType.DMA((sec_local,)),
            pltpu.SemaphoreType.DMA((count,)),
        ]
    else:
        out_shape = [jax.ShapeDtypeStruct((sec_local, packing.rows, TILE), BF16)]
        out_specs = [pl.BlockSpec(memory_space=pltpu.VMEM)]
    return pl.pallas_call(
        functools.partial(round_kernel, sec_local, phys_count, tiles, shared, final),
        out_shape=out_shape,
        in_specs=[smem, smem] + [anywhere] * (len(operands) - 2),
        out_specs=out_specs,
        scratch_shapes=scratch,
        name="last_round" if final else "round",
    )(*operands)


def body(tensors, factors, sector_sizes, merging):
    site_index = lax.axis_index("site")
    sec_index = lax.axis_index("sec")
    site_count = lax.axis_size("site")
    groups = lax.axis_size("sec")
    blocks = tensors[0]
    sec_local, phys_count, size = blocks.shape[0], blocks.shape[1], blocks.shape[3]
    count = sec_local * phys_count
    rows = lax.dynamic_index_in_dim(merging, site_index, 0, keepdims=False)
    next_widths = lax.dynamic_index_in_dim(
        sector_sizes, (site_index + 1) % site_count, 0, keepdims=False
    )
    first = sec_index * sec_local
    widths = lax.dynamic_slice_in_dim(next_widths, first, sec_local)
    slots = lax.dynamic_slice_in_dim(rows, first, sec_local).reshape(count) // sec_local
    wanted = rows[None] == (first + jnp.arange(sec_local, dtype=jnp.int32))[:, None, None]
    order = jnp.arange(rows.shape[0], dtype=jnp.int32)[None, :, None]
    lefts = jnp.sum(jnp.where(wanted, order, 0), axis=1).reshape(count)
    sources = lefts // sec_local

    def exchange(slotted):
        return lax.all_to_all(slotted, "sec", split_axis=0, concat_axis=0, tiled=True)

    first_slots = exchange(
        place_first(blocks.reshape(count, size, size), factors[0], slots, groups)
    )
    factor_slots = None
    for round_index in range(ROUNDS):
        final = round_index + 1 == ROUNDS
        outs = run_round(
            sources, widths, first_slots, factor_slots, sec_local, phys_count, size, final
        )
        if not final:
            packed = from_behind(outs[0], "site", 1)
            factor_slots = exchange(place(packed, slots, groups))
    isometry, upper = outs
    return isometry.reshape(1, sec_local, phys_count, size, size), upper[None]


def solution(mesh):
    in_specs = (P("site", "sec", None, None, None), P("site", "sec", None, None), P(), P())
    out_specs = (P("site", "sec", None, None, None), P("site", "sec", None, None))
    return jax.shard_map(body, mesh=mesh, in_specs=in_specs, out_specs=out_specs, check_vma=False)
```

time: 535 us -> 485 us (0.907); the launches traced: 534 us -> 476 us
  Pallas kernels: 179 us -> 146 us
  blocking collectives: 137 us -> 109 us
  waiting for transfers between devices: 191 us -> 206 us
  between operations: 14.1 us -> 1.22 us
    all_to_all x1, waiting for transfers between devices: 151 us -> 186 us  [exchange(): lax.all_to_all(slotted, 'sec', split_axis=0, concat_axis=0, tiled=True)]
    all_to_all x2, blocking collectives: 137 us -> 109 us  [exchange(): lax.all_to_all(slotted, 'sec', split_axis=0, concat_axis=0, tiled=True)]
    pallas_call x8 -> x4, Pallas kernels: 168 us -> 141 us  [the longest x3 134 us: run_round(): pl.pallas_call(functools.partial(round_kernel, sec_local, phys_count, til...]
    all_gather x1 -> x0, waiting for transfers between devices: 17.9 us -> none  [body(): factor_slots = lax.all_gather(packed, 'sec', axis=0, tiled=True)]
    pallas_call x3 -> x2, Pallas kernels: 10.6 us -> 4.88 us  [place(): pl.pallas_call(functools.partial(place_kernel, unique, count), out_shape=...]
  transfers between devices with their start and end apart: 4 -> 3, of which waited for: 4 -> 3; matrix products, arithmetic and copies ran while one was open for 1% -> 0% of each run, Pallas kernels for 1% -> 0%
where the time goes in v3:
time: 485 us; the launch traced here: 476 us
  waiting for transfers between devices  206 us (42%)
  Pallas kernels  146 us (30%)
  blocking collectives  109 us (22%)
  starting transfers between devices  8.13 us (2%)
    all_to_all x1, waiting for transfers between devices, exchange(): lax.all_to_all(slotted, 'sec', split_axis=0, concat_axis=0, tiled=True)  186 us
    pallas_call x3, Pallas kernels, run_round(): pl.pallas_call(functools.partial(round_kernel, sec_local, phys_count, til...  134 us
    all_to_all x2, blocking collectives, exchange(): lax.all_to_all(slotted, 'sec', split_axis=0, concat_axis=0, tiled=True)  109 us
    ppermute x2, waiting for transfers between devices, from_behind(): lax.ppermute(shard, axis, [(i, (i + by) % size) for i in range(size)])  20.2 us
  transfers between devices with their start and end apart: 3, of which 3 were waited for; matrix products, arithmetic and copies ran while one was open for 0% of the time, Pallas kernels for 0%

profile of v3, /device:TPU:0, one launch (start us, length us, event | category | flops | bytes accessed | tf_op | source)
XLA Modules:
  0.0 476.3 jit_solution(9315578801148490937)
XLA Ops:
  0.7 0.7 copy-done
  1.4 0.1 constant_dynamic-slice_fusion
  1.4 0.1 copy.8
  1.5 0.1 reshape.21
  1.6 0.5 and_select_fusion.slot_ref
  2.1 6.6 %place_first.1 = bf16[16,3088,128]{2,1,0:T(8,128)(2,1)} custom-call(s32[8]{0:T(128)} %and_select_fusion.slot_ref, f32[2,512,512]{2,1,0:T(8,128)} %bitcast.9, bf16[8,512,512]{2,1,0:T(8,128)(2,1)} %bitcast.8), custom_call_target="tpu_custom_call" | custom-call | tf_op jit(solution)/shard_map/place_first/pallas_call | solution.py:150
  8.7 8.1 %all-to-all-start = ((bf16[16,3088,128]{2,1,0:T(8,128)(2,1)}), bf16[16,3088,128]{2,1,0:T(8,128)(2,1)}, u32[]{:S(2)}, u32[]{:S(2)}) async-start(bf16[16,3088,128]{2,1,0:T(8,128)(2,1)} %place_first.1), calls=%async_computation | async-start | bytes 25296896 | tf_op jit(solution)/shard_map/all_to_all | solution.py:514
  16.9 0.2 select_reduce_fusion
  17.1 0.1 reshape.20
  17.2 1.3 dynamic-slice_bitcast_fusion.1.refs_1_
  18.5 0.5 and_select_fusion.1.refs_0_
  19.0 186.2 %all-to-all-done.refs_2_ = bf16[16,3088,128]{2,1,0:T(8,128)(2,1)} async-done(((bf16[16,3088,128]{2,1,0:T(8,128)(2,1)}), bf16[16,3088,128]{2,1,0:T(8,128)(2,1)}, u32[]{:S(2)}, u32[]{:S(2)}) %all-to-all-start) | async-done | bytes 12648480 | tf_op jit(solution)/shard_map/all_to_all | solution.py:514
  205.2 42.3 %round.2 = bf16[2,1040,128]{2,1,0:T(8,128)(2,1)} custom-call(s32[8]{0:T(128)} %and_select_fusion.1.refs_0_, s32[2]{0:T(128)} %dynamic-slice_bitcast_fusion.1.refs_1_, bf16[16,3088,128]{2,1,0:T(8,128)(2,1)} %all-to-all-done.refs_2_), custom_call_target="tpu_custom_call" | custom-call | tf_op jit(solution)/shard_map/round/pallas_call | solution.py:483
  247.5 0.0 collective-permute-start
  247.6 10.1 %collective-permute-done.block_ref = bf16[2,1040,128]{2,1,0:T(8,128)(2,1)S(1)} collective-permute-done((bf16[2,1040,128]{2,1,0:T(8,128)(2,1)}, bf16[2,1040,128]{2,1,0:T(8,128)(2,1)S(1)}, u32[]{:S(2)}, u32[]{:S(2)}) %collective-permute-start) | collective-permute-done | bytes 532512 | tf_op jit(solution)/shard_map/ppermute | solution.py:25
  257.7 0.8 copy-done.2
  258.5 2.4 place.2
  260.9 54.7 %all_to_all.15.refs_3_ = bf16[16,1040,128]{2,1,0:T(8,128)(2,1)} all-to-all(bf16[16,1040,128]{2,1,0:T(8,128)(2,1)} %place.2), channel_id=1, replica_groups=mesh['site'=8,'sec'=16] {'sec'}, dimensions={0} | all-to-all | bytes 8519680 | tf_op jit(solution)/shard_map/all_to_all | solution.py:514
  315.6 42.3 %round.3 = bf16[2,1040,128]{2,1,0:T(8,128)(2,1)} custom-call(s32[8]{0:T(128)} %and_select_fusion.1.refs_0_, s32[2]{0:T(128)} %dynamic-slice_bitcast_fusion.1.refs_1_, bf16[16,3088,128]{2,1,0:T(8,128)(2,1)} %all-to-all-done.refs_2_, bf16[16,1040,128]{2,1,0:T(8,128)(2,1)} %all_to_all.15.refs_3_), custom_call_target="tpu_custom_call" | custom-call | tf_op jit(solution)/shard_map/round/pallas_call | solution.py:483
  358.0 10.1 %collective-permute-done.1.block_ref = bf16[2,1040,128]{2,1,0:T(8,128)(2,1)S(1)} collective-permute-done((bf16[2,1040,128]{2,1,0:T(8,128)(2,1)}, bf16[2,1040,128]{2,1,0:T(8,128)(2,1)S(1)}, u32[]{:S(2)}, u32[]{:S(2)}) %collective-permute-start.1) | collective-permute-done | bytes 532512 | tf_op jit(solution)/shard_map/ppermute | solution.py:25
  368.1 0.8 copy-done.1
  368.9 2.4 place.3
  371.3 54.8 %all_to_all.16.refs_3_ = bf16[16,1040,128]{2,1,0:T(8,128)(2,1)} all-to-all(bf16[16,1040,128]{2,1,0:T(8,128)(2,1)} %place.3), channel_id=1, replica_groups=mesh['site'=8,'sec'=16] {'sec'}, dimensions={0} | all-to-all | bytes 8519680 | tf_op jit(solution)/shard_map/all_to_all | solution.py:514
  426.1 49.7 %last_round.1 = (f32[8,512,512]{2,1,0:T(8,128)}, f32[2,512,512]{2,1,0:T(8,128)}) custom-call(s32[8]{0:T(128)} %and_select_fusion.1.refs_0_, s32[2]{0:T(128)} %dynamic-slice_bitcast_fusion.1.refs_1_, bf16[16,3088,128]{2,1,0:T(8,128)(2,1)} %all-to-all-done.refs_2_, bf16[16,1040,128]{2,1,0:T(8,128)(2,1)} %all_to_all.16.refs_3_), custom_call_target="tpu_custom_call" | custom-call | tf_op jit(solution)/shard_map/last_round/pallas_call | solution.py:483
  (6 shorter events, 0.0 us)
Async XLA Ops:
  0.6 0.7 copy-start
  8.7 196.5 %all-to-all-start = ((bf16[16,3088,128]{2,1,0:T(8,128)(2,1)}), bf16[16,3088,128]{2,1,0:T(8,128)(2,1)}, u32[]{:S(2)}, u32[]{:S(2)}) async-start(bf16[16,3088,128]{2,1,0:T(8,128)(2,1)} %place_first.1), calls=%async_computation | async-start | bytes 25296896 | tf_op jit(solution)/shard_map/all_to_all | solution.py:514
  247.5 10.1 %collective-permute-start = (bf16[2,1040,128]{2,1,0:T(8,128)(2,1)}, bf16[2,1040,128]{2,1,0:T(8,128)(2,1)S(1)}, u32[]{:S(2)}, u32[]{:S(2)}) collective-permute-start(bf16[2,1040,128]{2,1,0:T(8,128)(2,1)} %round.2), channel_id=1, source_target_pairs={{0,16},{16,32},{32,48},{48,64},{64,80},{80,96},{96,112},{112,0},{1... | collective-permute-start | bytes 1597448 | tf_op jit(solution)/shard_map/ppermute | solution.py:25
  257.7 0.8 copy-start.2
  357.9 10.1 %collective-permute-start.1 = (bf16[2,1040,128]{2,1,0:T(8,128)(2,1)}, bf16[2,1040,128]{2,1,0:T(8,128)(2,1)S(1)}, u32[]{:S(2)}, u32[]{:S(2)}) collective-permute-start(bf16[2,1040,128]{2,1,0:T(8,128)(2,1)} %round.3), channel_id=1, source_target_pairs={{0,16},{16,32},{32,48},{48,64},{64,80},{80,96},{96,112},{112,0},{1... | collective-permute-start | bytes 1597448 | tf_op jit(solution)/shard_map/ppermute | solution.py:25
  368.1 0.8 copy-start.1

commit v4 on v3

--- a/solution.py
+++ b/solution.py
@@ -286,7 +286,7 @@
     row_id, column_id = ids()
     if final:
         isometry_ref, upper_out = outs
-        upper_ref, full, staged, upper_sem, isometry_sem = refs[7:]
+        upper_ref, full, high, low, staged, upper_sem, isometry_sem = refs[7:]
     else:
         packed_ref = outs[0]
     at_factor = tiles * size if shared else 0
@@ -328,9 +328,9 @@
 
     lax.fori_loop(0, count, multiply, 0)
     half = size // 2
-    for s in range(sec_local):
-        here = slice(s * phys_count, (s + 1) * phys_count)
-        stacked = products[here].reshape(phys_count * size, size)
+
+    def gram(s, carry):
+        stacked = products[pl.ds(s * phys_count, phys_count)].reshape(phys_count * size, size)
         work[s, :half, :] = contract(stacked[:, :half], stacked, 0, 0)
         work[s, half:, half:] = contract(stacked[:, half:], stacked[:, half:], 0, 0)
         for k in range(tiles):
@@ -339,6 +339,9 @@
             work[s, lo:hi, lo:hi] = work[s, lo:hi, lo:hi] + jnp.where(on, 1.0, 0.0)
         if final:
             upper_ref[s] = jnp.zeros((size, size), F32)
+        return carry
+
+    lax.fori_loop(0, sec_local, gram, 0)
 
     def step(p, carry):
         first = pl.multiple_of(p * TILE, TILE)
@@ -409,14 +412,12 @@
         ]
     )
     scale = math.sqrt(phys_count * size)
-    isometry_out = []
-    for s in range(sec_local):
+
+    def invert(s, carry):
         inverse = full.at[s]
         for k in range(tiles):
             lo, hi = k * TILE, (k + 1) * TILE
             inverse[lo:hi, lo:hi] = jnp.transpose(diag_inverse[s, lo:hi, :])
-            if k % 2 == 1:
-                inverse[lo:hi, lo - TILE : lo] = jnp.zeros((TILE, TILE), F32)
         span = TILE
         while span < size:
             for lo in range(0, size, 2 * span):
@@ -425,26 +426,32 @@
                     upper_ref[s, lo:mid, mid:hi], inverse[mid:hi, mid:hi], 1, 0, HIGHEST
                 )
                 inverse[lo:mid, mid:hi] = -contract(inverse[lo:mid, lo:mid], inner, 1, 0, HIGHEST)
-                if span > TILE:
-                    inverse[mid:hi, lo:mid] = jnp.zeros((span, span), F32)
+                inverse[mid:hi, lo:mid] = jnp.zeros((span, span), F32)
             span *= 2
-    for s in range(sec_local):
         scaled = full[s] * scale
-        high = scaled.astype(BF16)
-        low = (scaled - high.astype(F32)).astype(BF16)
-        for p in range(phys_count):
-            g = s * phys_count + p
-            for lo in range(0, size, 2 * TILE):
-                hi = lo + 2 * TILE
-                left = products[g, :, :hi]
-                staged[g, :, lo:hi] = contract(left, high[:hi, lo:hi], 1, 0) + contract(
-                    left, low[:hi, lo:hi], 1, 0
-                )
-            isometry_out.append(
-                pltpu.make_async_copy(staged.at[g], isometry_ref.at[g], isometry_sem.at[g])
+        rounded = scaled.astype(BF16)
+        high[s] = rounded
+        low[s] = (scaled - rounded.astype(F32)).astype(BF16)
+        return carry
+
+    lax.fori_loop(0, sec_local, invert, 0)
+
+    def isometry_copy(g):
+        return pltpu.make_async_copy(staged.at[g], isometry_ref.at[g], isometry_sem.at[g])
+
+    def multiply_back(g, carry):
+        s = g // phys_count
+        for lo in range(0, size, 2 * TILE):
+            hi = lo + 2 * TILE
+            left = products[g, :, :hi]
+            staged[g, :, lo:hi] = contract(left, high[s, :hi, lo:hi], 1, 0) + contract(
+                left, low[s, :hi, lo:hi], 1, 0
             )
-            isometry_out[-1].start()
-    wait_all(uppers_out + isometry_out)
+        isometry_copy(g).start()
+        return carry
+
+    lax.fori_loop(0, count, multiply_back, 0)
+    wait_all(uppers_out + [isometry_copy(g) for g in range(count)])
 
 
 def run_round(sources, widths, tensor_slots, factor_slots, sec_local, phys_count, size, final):
@@ -473,6 +480,8 @@
         scratch += [
             pltpu.VMEM((sec_local, size, size), F32),
             pltpu.VMEM((sec_local, size, size), F32),
+            pltpu.VMEM((sec_local, size, size), BF16),
+            pltpu.VMEM((sec_local, size, size), BF16),
             pltpu.VMEM((count, size, size), F32),
             pltpu.SemaphoreType.DMA((sec_local,)),
             pltpu.SemaphoreType.DMA((count,)),
@@ -508,7 +517,7 @@
     wanted = rows[None] == (first + jnp.arange(sec_local, dtype=jnp.int32))[:, None, None]
     order = jnp.arange(rows.shape[0], dtype=jnp.int32)[None, :, None]
     lefts = jnp.sum(jnp.where(wanted, order, 0), axis=1).reshape(count)
-    sources = lefts // sec_local
+    slots, sources, widths = lax.optimization_barrier((slots, lefts // sec_local, widths))
 
     def exchange(slotted):
         return lax.all_to_all(slotted, "sec", split_axis=0, concat_axis=0, tiled=True)

time: 485 us -> 433 us (0.89); the launches traced: 476 us -> 432 us
  waiting for transfers between devices: 206 us -> 20.2 us
  blocking collectives: 109 us -> 259 us
  starting transfers between devices: 8.13 us -> 0.03 us
    all_to_all x1 -> x0, waiting for transfers between devices: 186 us -> none  [exchange(): lax.all_to_all(slotted, 'sec', split_axis=0, concat_axis=0, tiled=True)]
    all_to_all x2 -> x3, blocking collectives: 109 us -> 259 us  [exchange(): lax.all_to_all(slotted, 'sec', split_axis=0, concat_axis=0, tiled=True)]
    all_to_all x1 -> x0, starting transfers between devices: 8.1 us -> none  [exchange(): lax.all_to_all(slotted, 'sec', split_axis=0, concat_axis=0, tiled=True)]
  transfers between devices with their start and end apart: 3 -> 2, of which waited for: 3 -> 2; matrix products, arithmetic and copies ran while one was open for 0% -> 0% of each run, Pallas kernels for 0% -> 0%
where the time goes in v4:
time: 433 us; the launch traced here: 432 us
  blocking collectives  259 us (60%)
  Pallas kernels  147 us (34%)
  waiting for transfers between devices  20.2 us (5%)
    all_to_all x3, blocking collectives, exchange(): lax.all_to_all(slotted, 'sec', split_axis=0, concat_axis=0, tiled=True)  259 us
    pallas_call x3, Pallas kernels, run_round(): pl.pallas_call(functools.partial(round_kernel, sec_local, phys_count, til...  136 us
    ppermute x2, waiting for transfers between devices, from_behind(): lax.ppermute(shard, axis, [(i, (i + by) % size) for i in range(size)])  20.2 us
  transfers between devices with their start and end apart: 2, of which 2 were waited for; matrix products, arithmetic and copies ran while one was open for 0% of the time, Pallas kernels for 0%

profile of v4, /device:TPU:0, one launch (start us, length us, event | category | flops | bytes accessed | tf_op | source)
XLA Modules:
  0.0 432.1 jit_solution(1909391256465465064)
XLA Ops:
  0.6 0.0 copy-start
  0.7 0.7 copy-done
  1.4 0.1 constant_dynamic-slice_fusion
  1.4 0.1 copy.8
  1.5 0.1 reshape.20
  1.6 0.2 select_reduce_fusion
  1.8 0.1 reshape.21
  1.9 1.3 dynamic-slice_bitcast_fusion.1.refs_1_
  3.2 0.6 and_select_fusion
  3.8 6.6 %place_first.1 = bf16[16,3088,128]{2,1,0:T(8,128)(2,1)} custom-call(s32[8]{0:T(128)} %get-tuple-element.9.slot_ref, f32[2,512,512]{2,1,0:T(8,128)} %bitcast.9, bf16[8,512,512]{2,1,0:T(8,128)(2,1)} %bitcast.8), custom_call_target="tpu_custom_call" | custom-call | tf_op jit(solution)/shard_map/place_first/pallas_call | solution.py:150
  10.4 149.6 %all_to_all.15.refs_2_ = bf16[16,3088,128]{2,1,0:T(8,128)(2,1)} all-to-all(bf16[16,3088,128]{2,1,0:T(8,128)(2,1)} %place_first.1), channel_id=1, replica_groups=mesh['site'=8,'sec'=16] {'sec'}, dimensions={0} | all-to-all | bytes 25296896 | tf_op jit(solution)/shard_map/all_to_all | solution.py:523
  160.0 42.5 %round.2 = bf16[2,1040,128]{2,1,0:T(8,128)(2,1)} custom-call(s32[8]{0:T(128)} %get-tuple-element.7.refs_0_, s32[2]{0:T(128)} %dynamic-slice_bitcast_fusion.1.refs_1_, bf16[16,3088,128]{2,1,0:T(8,128)(2,1)} %all_to_all.15.refs_2_), custom_call_target="tpu_custom_call" | custom-call | tf_op jit(solution)/shard_map/round/pallas_call | solution.py:492
  202.5 0.0 collective-permute-start
  202.6 10.1 %collective-permute-done.block_ref = bf16[2,1040,128]{2,1,0:T(8,128)(2,1)S(1)} collective-permute-done((bf16[2,1040,128]{2,1,0:T(8,128)(2,1)}, bf16[2,1040,128]{2,1,0:T(8,128)(2,1)S(1)}, u32[]{:S(2)}, u32[]{:S(2)}) %collective-permute-start) | collective-permute-done | bytes 532512 | tf_op jit(solution)/shard_map/ppermute | solution.py:25
  212.7 0.8 copy-done.2
  213.5 2.4 place.2
  215.9 56.3 %all_to_all.16.refs_3_ = bf16[16,1040,128]{2,1,0:T(8,128)(2,1)} all-to-all(bf16[16,1040,128]{2,1,0:T(8,128)(2,1)} %place.2), channel_id=1, replica_groups=mesh['site'=8,'sec'=16] {'sec'}, dimensions={0} | all-to-all | bytes 8519680 | tf_op jit(solution)/shard_map/all_to_all | solution.py:523
  272.2 42.5 %round.3 = bf16[2,1040,128]{2,1,0:T(8,128)(2,1)} custom-call(s32[8]{0:T(128)} %get-tuple-element.7.refs_0_, s32[2]{0:T(128)} %dynamic-slice_bitcast_fusion.1.refs_1_, bf16[16,3088,128]{2,1,0:T(8,128)(2,1)} %all_to_all.15.refs_2_, bf16[16,1040,128]{2,1,0:T(8,128)(2,1)} %all_to_all.16.refs_3_), custom_call_target="tpu_custom_call" | custom-call | tf_op jit(solution)/shard_map/round/pallas_call | solution.py:492
  314.7 0.0 collective-permute-start.1
  314.7 10.1 %collective-permute-done.1.block_ref = bf16[2,1040,128]{2,1,0:T(8,128)(2,1)S(1)} collective-permute-done((bf16[2,1040,128]{2,1,0:T(8,128)(2,1)}, bf16[2,1040,128]{2,1,0:T(8,128)(2,1)S(1)}, u32[]{:S(2)}, u32[]{:S(2)}) %collective-permute-start.1) | collective-permute-done | bytes 532512 | tf_op jit(solution)/shard_map/ppermute | solution.py:25
  324.8 0.8 copy-done.1
  325.6 2.4 place.3
  328.1 53.0 %all_to_all.17.refs_3_ = bf16[16,1040,128]{2,1,0:T(8,128)(2,1)} all-to-all(bf16[16,1040,128]{2,1,0:T(8,128)(2,1)} %place.3), channel_id=1, replica_groups=mesh['site'=8,'sec'=16] {'sec'}, dimensions={0} | all-to-all | bytes 8519680 | tf_op jit(solution)/shard_map/all_to_all | solution.py:523
  381.1 50.8 %last_round.1 = (f32[8,512,512]{2,1,0:T(8,128)}, f32[2,512,512]{2,1,0:T(8,128)}) custom-call(s32[8]{0:T(128)} %get-tuple-element.7.refs_0_, s32[2]{0:T(128)} %dynamic-slice_bitcast_fusion.1.refs_1_, bf16[16,3088,128]{2,1,0:T(8,128)(2,1)} %all_to_all.15.refs_2_, bf16[16,1040,128]{2,1,0:T(8,128)(2,1)} %all_to_all.17.refs_3_), custom_call_target="tpu_custom_call" | custom-call | tf_op jit(solution)/shard_map/last_round/pallas_call | solution.py:492
  (4 shorter events, 0.0 us)
Async XLA Ops:
  0.6 0.7 copy-start
  202.5 10.1 %collective-permute-start = (bf16[2,1040,128]{2,1,0:T(8,128)(2,1)}, bf16[2,1040,128]{2,1,0:T(8,128)(2,1)S(1)}, u32[]{:S(2)}, u32[]{:S(2)}) collective-permute-start(bf16[2,1040,128]{2,1,0:T(8,128)(2,1)} %round.2), channel_id=1, source_target_pairs={{0,16},{16,32},{32,48},{48,64},{64,80},{80,96},{96,112},{112,0},{1... | collective-permute-start | bytes 1597448 | tf_op jit(solution)/shard_map/ppermute | solution.py:25
  212.7 0.8 copy-start.2
  314.7 10.1 %collective-permute-start.1 = (bf16[2,1040,128]{2,1,0:T(8,128)(2,1)}, bf16[2,1040,128]{2,1,0:T(8,128)(2,1)S(1)}, u32[]{:S(2)}, u32[]{:S(2)}) collective-permute-start(bf16[2,1040,128]{2,1,0:T(8,128)(2,1)} %round.3), channel_id=1, source_target_pairs={{0,16},{16,32},{32,48},{48,64},{64,80},{80,96},{96,112},{112,0},{1... | collective-permute-start | bytes 1597448 | tf_op jit(solution)/shard_map/ppermute | solution.py:25
  324.8 0.8 copy-start.1

commit v5 on v4

--- a/solution.py
+++ b/solution.py
@@ -12,6 +12,7 @@
 F32 = jnp.float32
 BF16 = jnp.bfloat16
 TILE = 128
+BLOCK = 32
 HIGHEST = lax.Precision.HIGHEST
 
 
@@ -197,10 +198,10 @@
     )(slots, blocks)
 
 
-def factor_group(rows8, j, lane, sub):
+def factor_group(rows8, units8, j, lane, sub):
     full = (8, TILE)
     rows = [jnp.broadcast_to(rows8[t : t + 1, :], full) for t in range(8)]
-    units = [jnp.where(lane == j + t, 1.0, 0.0) for t in range(8)]
+    units = [jnp.broadcast_to(units8[t : t + 1, :], full) for t in range(8)]
     columns = [jnp.broadcast_to(rows8[:, j + u : j + u + 1], full) for u in range(8)]
     block = [
         [jnp.broadcast_to(columns[u][t : t + 1, :], full) if u >= t else None for u in range(8)]
@@ -225,30 +226,39 @@
         upper = jnp.where(sub == t, rows[t] * root, upper)
         unit = jnp.where(sub == t, units[t] * root, unit)
     reduced = [rows[t] * inverse[t] for t in range(8)]
+    reduced_units = [units[t] * inverse[t] for t in range(8)]
     for t in range(7, -1, -1):
         for v in range(t + 1, 8):
             reduced[t] = reduced[t] - lower[v, t] * reduced[v]
-    return upper, unit, reduced
+            reduced_units[t] = reduced_units[t] - lower[v, t] * reduced_units[v]
+    return upper, unit, reduced, reduced_units
 
 
 def factor_tile(stacks):
-    groups, wide = TILE // 8, 4
+    groups, wide = TILE // 8, BLOCK // 8
     lane = lax.broadcasted_iota(jnp.int32, (8, TILE), 1)
     sub = lax.broadcasted_iota(jnp.int32, (8, TILE), 0)
     uppers, units = [[] for _ in stacks], [[] for _ in stacks]
+    eyes = [[jnp.where(lane == 8 * i + sub, 1.0, 0.0) for i in range(groups)] for _ in stacks]
     for group in range(groups):
         j = group * 8
         end = (group // wide + 1) * wide
         for s, stack in enumerate(stacks):
-            upper, unit, reduced = factor_group(stack[group], j, lane, sub)
+            eye = eyes[s]
+            upper, unit, reduced, reduced_units = factor_group(
+                stack[group], eye[group], j, lane, sub
+            )
             uppers[s].append(upper)
             units[s].append(unit)
             for i in range(group + 1, end):
-                total = None
+                total, total_unit = None, None
                 for t in range(8):
-                    term = jnp.broadcast_to(stack[i][:, j + t : j + t + 1], (8, TILE)) * reduced[t]
+                    column = jnp.broadcast_to(stack[i][:, j + t : j + t + 1], (8, TILE))
+                    term, term_unit = column * reduced[t], column * reduced_units[t]
                     total = term if total is None else total + term
+                    total_unit = term_unit if total_unit is None else total_unit + term_unit
                 stack[i] = stack[i] - total
+                eye[i] = eye[i] - total_unit
         if end == group + 1 and end < groups:
             for s, stack in enumerate(stacks):
                 done = jnp.concatenate(uppers[s][end - wide :], axis=0)
@@ -259,7 +269,7 @@
 
 
 def invert_tiles(uppers, units, row_id, column_id):
-    span = 8
+    span = BLOCK
     while span < TILE:
         pair = (row_id // (2 * span) == column_id // (2 * span)) & (
             row_id // span != column_id // span

time: 433 us -> 421 us (0.972)
  Pallas kernels: 147 us -> 136 us
    pallas_call x3, Pallas kernels: 136 us -> 124 us  [run_round(): pl.pallas_call(functools.partial(round_kernel, sec_local, phys_count, til...]
where the time goes in v5:
time: 421 us
  blocking collectives  259 us (62%)
  Pallas kernels  136 us (32%)
  waiting for transfers between devices  20.2 us (5%)
    all_to_all x3, blocking collectives, exchange(): lax.all_to_all(slotted, 'sec', split_axis=0, concat_axis=0, tiled=True)  259 us
    pallas_call x3, Pallas kernels, run_round(): pl.pallas_call(functools.partial(round_kernel, sec_local, phys_count, til...  124 us
    ppermute x2, waiting for transfers between devices, from_behind(): lax.ppermute(shard, axis, [(i, (i + by) % size) for i in range(size)])  20.2 us
  transfers between devices with their start and end apart: 2, of which 2 were waited for; matrix products, arithmetic and copies ran while one was open for 0% of the time, Pallas kernels for 0%

profile of v5, /device:TPU:0, one launch (start us, length us, event | category | flops | bytes accessed | tf_op | source)
XLA Modules:
  0.0 420.5 jit_solution(15544363613428423330)
XLA Ops:
  0.6 0.0 copy-start
  0.7 0.7 copy-done
  1.4 0.1 constant_dynamic-slice_fusion
  1.4 0.1 copy.8
  1.5 0.1 reshape.20
  1.6 0.2 select_reduce_fusion
  1.8 0.1 reshape.21
  1.9 1.3 dynamic-slice_bitcast_fusion.1.refs_1_
  3.2 0.6 and_select_fusion
  3.8 6.6 %place_first.1 = bf16[16,3088,128]{2,1,0:T(8,128)(2,1)} custom-call(s32[8]{0:T(128)} %get-tuple-element.9.slot_ref, f32[2,512,512]{2,1,0:T(8,128)} %bitcast.9, bf16[8,512,512]{2,1,0:T(8,128)(2,1)} %bitcast.8), custom_call_target="tpu_custom_call" | custom-call | tf_op jit(solution)/shard_map/place_first/pallas_call | solution.py:151
  10.4 149.7 %all_to_all.15.refs_2_ = bf16[16,3088,128]{2,1,0:T(8,128)(2,1)} all-to-all(bf16[16,3088,128]{2,1,0:T(8,128)(2,1)} %place_first.1), channel_id=1, replica_groups=mesh['site'=8,'sec'=16] {'sec'}, dimensions={0} | all-to-all | bytes 25296896 | tf_op jit(solution)/shard_map/all_to_all | solution.py:533
  160.1 38.7 %round.2 = bf16[2,1040,128]{2,1,0:T(8,128)(2,1)} custom-call(s32[8]{0:T(128)} %get-tuple-element.7.refs_0_, s32[2]{0:T(128)} %dynamic-slice_bitcast_fusion.1.refs_1_, bf16[16,3088,128]{2,1,0:T(8,128)(2,1)} %all_to_all.15.refs_2_), custom_call_target="tpu_custom_call" | custom-call | tf_op jit(solution)/shard_map/round/pallas_call | solution.py:502
  198.8 0.0 collective-permute-start
  198.8 10.1 %collective-permute-done.block_ref = bf16[2,1040,128]{2,1,0:T(8,128)(2,1)S(1)} collective-permute-done((bf16[2,1040,128]{2,1,0:T(8,128)(2,1)}, bf16[2,1040,128]{2,1,0:T(8,128)(2,1)S(1)}, u32[]{:S(2)}, u32[]{:S(2)}) %collective-permute-start) | collective-permute-done | bytes 532512 | tf_op jit(solution)/shard_map/ppermute | solution.py:26
  208.9 0.8 copy-done.2
  209.7 2.4 place.2
  212.1 56.0 %all_to_all.16.refs_3_ = bf16[16,1040,128]{2,1,0:T(8,128)(2,1)} all-to-all(bf16[16,1040,128]{2,1,0:T(8,128)(2,1)} %place.2), channel_id=1, replica_groups=mesh['site'=8,'sec'=16] {'sec'}, dimensions={0} | all-to-all | bytes 8519680 | tf_op jit(solution)/shard_map/all_to_all | solution.py:533
  268.2 38.7 %round.3 = bf16[2,1040,128]{2,1,0:T(8,128)(2,1)} custom-call(s32[8]{0:T(128)} %get-tuple-element.7.refs_0_, s32[2]{0:T(128)} %dynamic-slice_bitcast_fusion.1.refs_1_, bf16[16,3088,128]{2,1,0:T(8,128)(2,1)} %all_to_all.15.refs_2_, bf16[16,1040,128]{2,1,0:T(8,128)(2,1)} %all_to_all.16.refs_3_), custom_call_target="tpu_custom_call" | custom-call | tf_op jit(solution)/shard_map/round/pallas_call | solution.py:502
  306.8 0.0 collective-permute-start.1
  306.9 10.1 %collective-permute-done.1.block_ref = bf16[2,1040,128]{2,1,0:T(8,128)(2,1)S(1)} collective-permute-done((bf16[2,1040,128]{2,1,0:T(8,128)(2,1)}, bf16[2,1040,128]{2,1,0:T(8,128)(2,1)S(1)}, u32[]{:S(2)}, u32[]{:S(2)}) %collective-permute-start.1) | collective-permute-done | bytes 532512 | tf_op jit(solution)/shard_map/ppermute | solution.py:26
  317.0 0.8 copy-done.1
  317.8 2.4 place.3
  320.2 53.2 %all_to_all.17.refs_3_ = bf16[16,1040,128]{2,1,0:T(8,128)(2,1)} all-to-all(bf16[16,1040,128]{2,1,0:T(8,128)(2,1)} %place.3), channel_id=1, replica_groups=mesh['site'=8,'sec'=16] {'sec'}, dimensions={0} | all-to-all | bytes 8519680 | tf_op jit(solution)/shard_map/all_to_all | solution.py:533
  373.4 46.9 %last_round.1 = (f32[8,512,512]{2,1,0:T(8,128)}, f32[2,512,512]{2,1,0:T(8,128)}) custom-call(s32[8]{0:T(128)} %get-tuple-element.7.refs_0_, s32[2]{0:T(128)} %dynamic-slice_bitcast_fusion.1.refs_1_, bf16[16,3088,128]{2,1,0:T(8,128)(2,1)} %all_to_all.15.refs_2_, bf16[16,1040,128]{2,1,0:T(8,128)(2,1)} %all_to_all.17.refs_3_), custom_call_target="tpu_custom_call" | custom-call | tf_op jit(solution)/shard_map/last_round/pallas_call | solution.py:502
  (4 shorter events, 0.0 us)
Async XLA Ops:
  0.6 0.7 copy-start
  198.8 10.1 %collective-permute-start = (bf16[2,1040,128]{2,1,0:T(8,128)(2,1)}, bf16[2,1040,128]{2,1,0:T(8,128)(2,1)S(1)}, u32[]{:S(2)}, u32[]{:S(2)}) collective-permute-start(bf16[2,1040,128]{2,1,0:T(8,128)(2,1)} %round.2), channel_id=1, source_target_pairs={{0,16},{16,32},{32,48},{48,64},{64,80},{80,96},{96,112},{112,0},{1... | collective-permute-start | bytes 1597448 | tf_op jit(solution)/shard_map/ppermute | solution.py:26
  208.9 0.8 copy-start.2
  306.8 10.1 %collective-permute-start.1 = (bf16[2,1040,128]{2,1,0:T(8,128)(2,1)}, bf16[2,1040,128]{2,1,0:T(8,128)(2,1)S(1)}, u32[]{:S(2)}, u32[]{:S(2)}) collective-permute-start(bf16[2,1040,128]{2,1,0:T(8,128)(2,1)} %round.3), channel_id=1, source_target_pairs={{0,16},{16,32},{32,48},{48,64},{64,80},{80,96},{96,112},{112,0},{1... | collective-permute-start | bytes 1597448 | tf_op jit(solution)/shard_map/ppermute | solution.py:26
  317.0 0.8 copy-start.1

commit v6 on v5

--- a/solution.py
+++ b/solution.py
@@ -162,6 +162,7 @@
             pltpu.SemaphoreType.DMA((count, tiles)),
             pltpu.SemaphoreType.DMA((count,)),
         ],
+        compiler_params=pltpu.CompilerParams(vmem_limit_bytes=16 * 2**20),
         name="place_first",
     )(slots, factors, blocks)
 
@@ -194,6 +195,7 @@
         scratch_shapes=[
             pltpu.SemaphoreType.DMA((count,)),
         ],
+        compiler_params=pltpu.CompilerParams(vmem_limit_bytes=8 * 2**20),
         name="place",
     )(slots, blocks)
 
@@ -288,15 +290,20 @@
     source_ref, width_ref, tensor_slots = refs[:3]
     factor_slots = tensor_slots if shared else refs[3]
     refs = refs[3 if shared else 4 :]
-    outs, refs = refs[: 2 if final else 1], refs[2 if final else 1 :]
-    tensors, factors, products, work, diag_inverse, tensor_sem, factor_sem = refs[:7]
+    n_outs = 2 if final or shared else 1
+    outs, refs = refs[:n_outs], refs[n_outs:]
+    if shared:
+        tensors = outs[1]
+    else:
+        tensors = tensor_slots
+    factors, products, work, diag_inverse, tensor_sem, factor_sem = refs[:6]
     packing = Packing(tiles)
     size = tiles * TILE
     count = sec_local * phys_count
     row_id, column_id = ids()
     if final:
         isometry_ref, upper_out = outs
-        upper_ref, full, high, low, staged, upper_sem, isometry_sem = refs[7:]
+        upper_ref, full, high, low, staged, upper_sem, isometry_sem = refs[6:]
     else:
         packed_ref = outs[0]
     at_factor = tiles * size if shared else 0
@@ -317,13 +324,15 @@
 
     for g in range(count):
         factor_copy(g).start()
-        for q in range(tiles):
-            tensor_copy(g, q).start()
+        if shared:
+            for q in range(tiles):
+                tensor_copy(g, q).start()
 
     def multiply(g, carry):
         factor_copy(g).wait()
-        for q in range(tiles):
-            tensor_copy(g, q).wait()
+        if shared:
+            for q in range(tiles):
+                tensor_copy(g, q).wait()
         held = factors.at[g]
         diagonal = unpack_diagonals(packing, held, row_id, column_id)
         for k in range(tiles):
@@ -470,10 +479,10 @@
     count = sec_local * phys_count
     anywhere = pl.BlockSpec(memory_space=pl.ANY)
     smem = pl.BlockSpec(memory_space=pltpu.SMEM)
+    vmem = pl.BlockSpec(memory_space=pltpu.VMEM)
     shared = factor_slots is None
     operands = [sources, widths, tensor_slots] + ([] if shared else [factor_slots])
     scratch = [
-        pltpu.VMEM((count, size, size), BF16),
         pltpu.VMEM((count, packing.rows, TILE), BF16),
         pltpu.VMEM((count, size, size), BF16),
         pltpu.VMEM((sec_local, size, size), F32),
@@ -499,12 +508,16 @@
     else:
         out_shape = [jax.ShapeDtypeStruct((sec_local, packing.rows, TILE), BF16)]
         out_specs = [pl.BlockSpec(memory_space=pltpu.VMEM)]
+        if shared:
+            out_shape.append(pltpu.VMEM((count, size, size), BF16))
+            out_specs.append(pl.BlockSpec(memory_space=pltpu.VMEM))
     return pl.pallas_call(
         functools.partial(round_kernel, sec_local, phys_count, tiles, shared, final),
         out_shape=out_shape,
-        in_specs=[smem, smem] + [anywhere] * (len(operands) - 2),
+        in_specs=[smem, smem] + ([anywhere] if shared else [vmem, anywhere]),
         out_specs=out_specs,
         scratch_shapes=scratch,
+        compiler_params=pltpu.CompilerParams(vmem_limit_bytes=40 * 2**20),
         name="last_round" if final else "round",
     )(*operands)
 
@@ -541,6 +554,8 @@
         outs = run_round(
             sources, widths, first_slots, factor_slots, sec_local, phys_count, size, final
         )
+        if round_index == 0:
+            first_slots = outs[1]
         if not final:
             packed = from_behind(outs[0], "site", 1)
             factor_slots = exchange(place(packed, slots, groups))

time: 421 us -> 406 us (0.964)
  Pallas kernels: 136 us -> 123 us
    pallas_call x3, Pallas kernels: 124 us -> 119 us  [run_round(): pl.pallas_call(functools.partial(round_kernel, sec_local, phys_count, til...]
where the time goes in v6:
time: 406 us; the launch traced here: 405 us
  blocking collectives  256 us (63%)
  Pallas kernels  123 us (30%)
  waiting for transfers between devices  19.8 us (5%)
  local copies, waits for them, and re-layouts  5.55 us (1%)
    all_to_all x3, blocking collectives, exchange(): lax.all_to_all(slotted, 'sec', split_axis=0, concat_axis=0, tiled=True)  256 us
    pallas_call x3, Pallas kernels, run_round(): pl.pallas_call(functools.partial(round_kernel, sec_local, phys_count, til...  119 us
    ppermute x2, waiting for transfers between devices, from_behind(): lax.ppermute(shard, axis, [(i, (i + by) % size) for i in range(size)])  19.8 us
  transfers between devices with their start and end apart: 2, of which 2 were waited for; matrix products, arithmetic and copies ran while one was open for 0% of the time, Pallas kernels for 0%

profile of v6, /device:TPU:0, one launch (start us, length us, event | category | flops | bytes accessed | tf_op | source)
XLA Modules:
  0.0 405.3 jit_solution(15679385272828876383)
XLA Ops:
  0.6 0.0 copy-start
  0.7 0.7 copy-done
  1.4 0.1 constant_dynamic-slice_fusion
  1.4 0.1 copy.8
  1.5 0.1 reshape.20
  1.6 0.2 select_reduce_fusion
  1.8 0.1 reshape.21
  1.9 0.8 dynamic-slice_bitcast_fusion.1.refs_1_
  2.7 0.0 copy-start.1
  2.7 2.2 copy-done.1
  4.9 1.6 copy-done.2
  6.5 2.7 place_first.1
  9.2 149.5 %all_to_all.15.refs_2_ = bf16[16,3088,128]{2,1,0:T(8,128)(2,1)} all-to-all(bf16[16,3088,128]{2,1,0:T(8,128)(2,1)S(1)} %place_first.1), channel_id=1, replica_groups=mesh['site'=8,'sec'=16] {'sec'}, dimensions={0} | all-to-all | bytes 25296896 | tf_op jit(solution)/shard_map/all_to_all | solution.py:546
  158.7 37.8 %round.2 = (bf16[2,1040,128]{2,1,0:T(8,128)(2,1)S(1)}, bf16[8,512,512]{2,1,0:T(8,128)(2,1)S(1)}) custom-call(s32[8]{0:T(128)S(1)} %get-tuple-element.9.refs_0_, s32[2]{0:T(128)S(1)} %dynamic-slice_bitcast_fusion.1.refs_1_, bf16[16,3088,128]{2,1,0:T(8,128)(2,1)} %all_to_all.15.refs_2_), custom_call_target="tpu_custom_call" | custom-call | tf_op jit(solution)/shard_map/round/pallas_call | solution.py:514
  196.5 0.0 collective-permute-start
  196.5 9.9 %collective-permute-done.block_ref = bf16[2,1040,128]{2,1,0:T(8,128)(2,1)S(1)} collective-permute-done((bf16[2,1040,128]{2,1,0:T(8,128)(2,1)S(1)}, bf16[2,1040,128]{2,1,0:T(8,128)(2,1)S(1)}, u32[]{:S(2)}, u32[]{:S(2)}) %collective-permute-start) | collective-permute-done | bytes 532512 | tf_op jit(solution)/shard_map/ppermute | solution.py:26
  206.4 0.8 place.2
  207.2 53.1 %all_to_all.16.refs_3_ = bf16[16,1040,128]{2,1,0:T(8,128)(2,1)S(1)} all-to-all(bf16[16,1040,128]{2,1,0:T(8,128)(2,1)S(1)} %place.2), channel_id=1, replica_groups=mesh['site'=8,'sec'=16] {'sec'}, dimensions={0} | all-to-all | bytes 8519680 | tf_op jit(solution)/shard_map/all_to_all | solution.py:546
  260.3 35.9 %round.3 = bf16[2,1040,128]{2,1,0:T(8,128)(2,1)S(1)} custom-call(s32[8]{0:T(128)S(1)} %get-tuple-element.9.refs_0_, s32[2]{0:T(128)S(1)} %dynamic-slice_bitcast_fusion.1.refs_1_, bf16[8,512,512]{2,1,0:T(8,128)(2,1)S(1)} %get-tuple-element.12.refs_2_, bf16[16,1040,128]{2,1,0:T(8,128)(2,1)S(1)} %all_to_all.16.refs_3_), custom_call_target="tpu_custom_call" | custom-call | tf_op jit(solution)/shard_map/round/pallas_call | solution.py:514
  296.3 0.0 collective-permute-start.1
  296.3 9.9 %collective-permute-done.1.block_ref = bf16[2,1040,128]{2,1,0:T(8,128)(2,1)S(1)} collective-permute-done((bf16[2,1040,128]{2,1,0:T(8,128)(2,1)S(1)}, bf16[2,1040,128]{2,1,0:T(8,128)(2,1)S(1)}, u32[]{:S(2)}, u32[]{:S(2)}) %collective-permute-start.1) | collective-permute-done | bytes 532512 | tf_op jit(solution)/shard_map/ppermute | solution.py:26
  306.2 0.8 place.3
  307.0 53.1 %all_to_all.17.refs_3_ = bf16[16,1040,128]{2,1,0:T(8,128)(2,1)S(1)} all-to-all(bf16[16,1040,128]{2,1,0:T(8,128)(2,1)S(1)} %place.3), channel_id=1, replica_groups=mesh['site'=8,'sec'=16] {'sec'}, dimensions={0} | all-to-all | bytes 8519680 | tf_op jit(solution)/shard_map/all_to_all | solution.py:546
  360.2 45.0 %last_round.1 = (f32[8,512,512]{2,1,0:T(8,128)}, f32[2,512,512]{2,1,0:T(8,128)}) custom-call(s32[8]{0:T(128)S(1)} %get-tuple-element.9.refs_0_, s32[2]{0:T(128)S(1)} %dynamic-slice_bitcast_fusion.1.refs_1_, bf16[8,512,512]{2,1,0:T(8,128)(2,1)S(1)} %get-tuple-element.12.refs_2_, bf16[16,1040,128]{2,1,0:T(8,128)(2,1)S(1)} %all_to_all.17.refs_3_), custom_call_target="tpu_custom_call" | custom-call | tf_op jit(solution)/shard_map/last_round/pallas_call | solution.py:514
  (4 shorter events, 0.0 us)
Async XLA Ops:
  0.6 0.7 copy-start
  2.7 2.2 copy-start.1
  4.9 1.6 copy-start.2
  196.5 9.9 %collective-permute-start = (bf16[2,1040,128]{2,1,0:T(8,128)(2,1)S(1)}, bf16[2,1040,128]{2,1,0:T(8,128)(2,1)S(1)}, u32[]{:S(2)}, u32[]{:S(2)}) collective-permute-start(bf16[2,1040,128]{2,1,0:T(8,128)(2,1)S(1)} %get-tuple-element.13), channel_id=1, source_target_pairs={{0,16},{16,32},{32,48},{48,64},{64,80},{80,96},{96,112},{112,0},{1... | collective-permute-start | bytes 1597448 | tf_op jit(solution)/shard_map/ppermute | solution.py:26
  296.3 9.9 %collective-permute-start.1 = (bf16[2,1040,128]{2,1,0:T(8,128)(2,1)S(1)}, bf16[2,1040,128]{2,1,0:T(8,128)(2,1)S(1)}, u32[]{:S(2)}, u32[]{:S(2)}) collective-permute-start(bf16[2,1040,128]{2,1,0:T(8,128)(2,1)S(1)} %round.3), channel_id=1, source_target_pairs={{0,16},{16,32},{32,48},{48,64},{64,80},{80,96},{96,112},{112,0},{1... | collective-permute-start | bytes 1597448 | tf_op jit(solution)/shard_map/ppermute | solution.py:26
